TPU v7x, 512 devices: a whole 4x4x16 slice. The times are simulated.
512 devices in a mesh: gx: 16 (over x, y), gy: 32 (over z, core).
Axes of the slice: x: 4, y: 4, z: 16, core: 2. Of those that a mesh axis runs over, the one named last changes fastest.
Arguments:
- conc: float32 [512, 256, 1024], P('gy', 'gx'), may hold values from 0.05 to 2
- target_one: float32 [512, 256, 1024], P('gy', 'gx'), may hold values from 0.05 to 5
- target_two: float32 [512, 256, 1024], P('gy', 'gx'), may hold values from 0.05 to 5
- diffusivity: float32 [512], replicated, may hold values from 2 to 200
- src_shift: int32 [512, 256, 8], P('gy', 'gx'), may hold values from 0 to 2, as said below
- src_tile: int32 [512, 256, 8], P('gy', 'gx'), may hold values from 0 to 2047
- interp_class: int32 [512, 256, 8], P('gy', 'gx'), may hold values from 0 to 7
- interp_mats: float32 [8, 128, 128], replicated, may hold values from 0 to 1, as said below
Outputs:
- new_conc: float32 [512, 256, 1024], P('gy', 'gx')
Inputs may be any that keep to these rules, and one draw needn't show every extreme that they name: `src_shift`: on the device at gx index i every offset is at most i; on each device at most 512 tiles have offset 1 and at most 512 have offset 2, and some device has exactly 512 of each. `interp_mats`: each matrix is tridiagonal with nonnegative entries.
All inputs are finite; a program needn't handle non-finite values.
Results may differ from a plain program's by a relative error of at most 0.00025.
Values sent between devices are 32-bit elements; how exact they have to be, the bound alone decides.
No kernel may reach another device: no remote copies, remote signals or barrier semaphores. Data moves between devices by JAX's collectives and lax.ppermute only.
A program may use at most 64 MiB of HBM per device.

v0:
```python
import jax
import jax.numpy as jnp
from jax import lax
from jax.sharding import PartitionSpec as P

TILE = 128
NMAT = 8


def shifted(value, axis, by):
    peers = lax.axis_size(axis)
    pairs = [(i, i + by) for i in range(peers) if 0 <= i + by < peers]
    return lax.ppermute(value, axis, pairs)


def local(
    conc, target_one, target_two, diffusivity, src_shift, src_tile, interp_class, interp_mats
):
    z_slab, x_slab, y_cells = conc.shape
    tile_rows = conc.reshape(-1, TILE)
    shift_flat = src_shift.reshape(-1)
    tile_flat = src_tile.reshape(-1)
    layers = [tile_rows]
    for offset in (1, 2):
        layers.append(shifted(tile_rows, "gx", offset))
    stacked = jnp.stack(layers)
    departed = stacked[shift_flat, tile_flat]
    products = jnp.einsum("tm,gnm->tgn", departed, interp_mats, precision=lax.Precision.HIGHEST)
    matches = interp_class.reshape(-1)[:, None] == jnp.arange(NMAT, dtype=jnp.int32)[None, :]
    advected = jnp.sum(jnp.where(matches[:, :, None], products, 0.0), axis=1)
    advected = advected.reshape(z_slab, x_slab, y_cells)
    free_part = advected / (1.0 + target_one / (0.5 + advected) + target_two / (2.0 + advected))
    bound_part = advected - free_part
    face_coef = 0.5 * (diffusivity[1:] + diffusivity[:-1])
    zero_pad = jnp.zeros((1,), diffusivity.dtype)
    lower_band = jnp.concatenate([zero_pad, -face_coef])
    upper_band = jnp.concatenate([-face_coef, zero_pad])
    main_band = (
        1.0 + jnp.concatenate([zero_pad, face_coef]) + jnp.concatenate([face_coef, zero_pad])
    )
    pencil = lax.all_to_all(free_part, "gy", split_axis=2, concat_axis=0, tiled=True)
    depth, items, y_piece = pencil.shape
    solved = lax.linalg.tridiagonal_solve(
        lower_band, main_band, upper_band, pencil.reshape(depth, items * y_piece)
    )
    solved = lax.all_to_all(
        solved.reshape(depth, items, y_piece), "gy", split_axis=0, concat_axis=2, tiled=True
    )
    return solved + bound_part


def solution(mesh):
    in_specs = (
        P("gy", "gx", None),
        P("gy", "gx", None),
        P("gy", "gx", None),
        P(),
        P("gy", "gx", None),
        P("gy", "gx", None),
        P("gy", "gx", None),
        P(),
    )
    out_specs = P("gy", "gx", None)
    return jax.shard_map(local, mesh=mesh, in_specs=in_specs, out_specs=out_specs, check_vma=False)
```

profile of v0, /device:TPU:10, one launch (start us, length us, event | category | flops | bytes accessed | tf_op | source)
XLA Modules:
  0.0 2141.3 jit_solution(959313084081357247)
XLA Ops:
  29.5 43.6 %collective-permute-done.1 = f32[2048,128]{1,0:T(8,128)} collective-permute-done((f32[2048,128]{1,0:T(8,128)S(1)}, f32[2048,128]{1,0:T(8,128)}, u32[]{:S(2)}, u32[]{:S(2)}) %collective-permute-start.1) | collective-permute-done | bytes 1048608 | tf_op jit(solution)/shard_map/ppermute | solution.py:13
  76.5 20.5 gather_fusion
  143.0 51.1 %all-to-all-done = f32[32,1,8192]{2,1,0:T(1,128)} async-done(((f32[32,1,8192]{2,1,0:T(1,128)}), f32[32,1,8192]{2,1,0:T(1,128)}, u32[]{:S(2)}, u32[]{:S(2)}) %all-to-all-start) | async-done | bytes 1048608 | tf_op jit(solution)/shard_map/all_to_all | solution.py:41
  223.8 1317.2 %while.32 = (s32[]{:T(128)}, f32[]{:T(128)}, f32[512]{0:T(512)S(1)}, f32[15,32]{1,0:T(8,128)S(1)}, f32[15,32,512]{2,1,0:T(8,128)}, /*index=5*/f32[15,32]{1,0:T(8...) while((s32[]{:T(128)}, f32[]{:T(128)}, ...), condition=%wide.region_2.3_spmd, body=%wide.region_1.2_spmd.sunk | while | flops 49281 | bytes 535273 | solution.py:43
  289.8 20.1 subtract_divide_fusion.125
  377.6 20.1 subtract_divide_fusion.125
  465.4 20.1 subtract_divide_fusion.125
  553.2 20.1 subtract_divide_fusion.125
  641.1 20.1 subtract_divide_fusion.125
  728.9 20.1 subtract_divide_fusion.125
  816.7 20.1 subtract_divide_fusion.125
  904.6 20.1 subtract_divide_fusion.125
  992.4 20.1 subtract_divide_fusion.125
  1080.2 20.1 subtract_divide_fusion.125
  1168.0 20.1 subtract_divide_fusion.125
  1255.8 20.1 subtract_divide_fusion.125
  1343.6 20.1 subtract_divide_fusion.125
  1431.4 20.1 subtract_divide_fusion.125
  1519.2 20.1 subtract_divide_fusion.125
  1630.6 373.2 %while.33 = (s32[]{:T(128)}, f32[512]{0:T(512)S(1)}, f32[15,32,512]{2,1,0:T(8,128)}, f32[15,32,512]{2,1,0:T(8,128)}, f32[15,32]{1,0:T(8,128)S(1)}, /*index=5*/s3...) while((s32[]{:T(128)}, f32[512]{0:T(512)S(1)}, ...), condition=%wide.region_4.5_spmd, body=%wide.region_3.4_spmd.sunk | while | flops 32802 | bytes 531929 | solution.py:43
  1634.6 20.1 multiply_subtract_fusion.125
  1684.4 20.1 multiply_subtract_fusion.125
  1709.2 20.1 multiply_subtract_fusion.125
  2057.4 61.1 %all_to_all.33 = f32[32,1,8192]{2,1,0:T(1,128)} all-to-all(f32[32,1,8192]{2,1,0:T(1,128)} %reshape.596), channel_id=1, replica_groups=mesh['gx'=16,'gy'=32] {'gy'}, dimensions={0} | all-to-all | bytes 2097152 | tf_op jit(solution)/shard_map/all_to_all | solution.py:46
  (495 shorter events, 646.7 us)
Async XLA Ops:
  0.0 97.0 %copy-start = (f32[8,128,128]{2,1,0:T(8,128)S(1)}, f32[8,128,128]{2,1,0:T(8,128)}, u32[]{:S(2)}) copy-start(f32[8,128,128]{2,1,0:T(8,128)} %param.19) | copy-start | bytes 1572868
  0.0 10.1 copy-start.2
  0.0 10.4 copy-start.3
  0.0 10.6 copy-start.4
  1.5 28.0 %collective-permute-start = (f32[2048,128]{1,0:T(8,128)S(1)}, f32[2048,128]{1,0:T(8,128)}, u32[]{:S(2)}, u32[]{:S(2)}) collective-permute-start(f32[2048,128]{1,0:T(8,128)S(1)} %reshape.574), channel_id=1, source_target_pairs={{0,32},{32,64},{64,96},{96,128},{128,160},{160,192},{192,224},{224... | collective-permute-start | bytes 3145736 | tf_op jit(solution)/shard_map/ppermute | solution.py:13
  5.0 68.1 %collective-permute-start.1 = (f32[2048,128]{1,0:T(8,128)S(1)}, f32[2048,128]{1,0:T(8,128)}, u32[]{:S(2)}, u32[]{:S(2)}) collective-permute-start(f32[2048,128]{1,0:T(8,128)S(1)} %reshape.574), channel_id=1, source_target_pairs={{0,64},{32,96},{64,128},{96,160},{128,192},{160,224},{192,256},{22... | collective-permute-start | bytes 3145736 | tf_op jit(solution)/shard_map/ppermute | solution.py:13
  115.6 22.8 %copy-start.5 = (f32[512]{0:T(512)S(1)}, f32[512]{0:T(512)}, u32[]{:S(2)}) copy-start(f32[512]{0:T(512)} %param.15) | copy-start | bytes 6148
  122.5 71.6 %all-to-all-start = ((f32[32,1,8192]{2,1,0:T(1,128)}), f32[32,1,8192]{2,1,0:T(1,128)}, u32[]{:S(2)}, u32[]{:S(2)}) async-start(f32[32,1,8192]{2,1,0:T(1,128)} %reshape.594), calls=%async_computation | async-start | bytes 2097152 | tf_op jit(solution)/shard_map/all_to_all | solution.py:41
  2127.6 13.7 copy-start.1
where the time goes:
time: 2170 us; the launch traced here: 2140 us
  loops' own time  898 us (41%)
  other arithmetic  662 us (31%)
  local copies, waits for them, and re-layouts  317 us (15%)
  waiting for transfers between devices  113 us (5%)
  blocking collectives  61.1 us (3%)
  between operations  58.4 us (3%)
  starting transfers between devices  23.1 us (1%)
    another operation x2, loops' own time, local(): lax.linalg.tridiagonal_solve(lower_band, main_band, upper_band, pencil.re...  898 us
    div x16, other arithmetic, local(): lax.linalg.tridiagonal_solve(lower_band, main_band, upper_band, pencil.re...  321 us
    sub x16, other arithmetic, local(): lax.linalg.tridiagonal_solve(lower_band, main_band, upper_band, pencil.re...  320 us
    slice x194, local copies, waits for them, and re-layouts, local(): lax.linalg.tridiagonal_solve(lower_band, main_band, upper_band, pencil.re...  176 us
    ppermute x2, waiting for transfers between devices, shifted(): return lax.ppermute(value, axis, pairs)  62.2 us
    all_to_all x1, blocking collectives, local(): lax.all_to_all(solved.reshape(depth, items, y_piece), 'gy', split_axis=0,...  61.1 us
    all_to_all x1, waiting for transfers between devices, local(): lax.all_to_all(free_part, 'gy', split_axis=2, concat_axis=0, tiled=True)  51.1 us
  transfers between devices with their start and end apart: 3, of which 3 were waited for; matrix products, arithmetic and copies ran while one was open for 0% of the time, Pallas kernels for 0%

commit v1 on v0

v1 whole, which is shorter than its diff:
```python
import functools

import jax
import jax.numpy as jnp
from jax import lax
from jax.experimental import pallas as pl
from jax.experimental.pallas import tpu as pltpu
from jax.sharding import PartitionSpec as P

LANES = 128
NMAT = 8
PLANES = 16
ROWS = 128
TILES = PLANES * ROWS
CAP = 512
HIGH = lax.Precision.HIGHEST
VMEM = pltpu.VMEM
SMEM = pltpu.SMEM


def shifted(value, axis, by):
    peers = lax.axis_size(axis)
    pairs = [(i, i + by) for i in range(peers) if 0 <= i + by < peers]
    return lax.ppermute(value, axis, pairs)


def to_rows(value):
    z, x, y = value.shape
    value = value.reshape(z, x // 8, 8, y // LANES, LANES).transpose(0, 1, 3, 2, 4)
    return value.reshape(z * x * (y // LANES), LANES)


def from_rows(rows, shape):
    z, x, y = shape
    rows = rows.reshape(z, x // 8, y // LANES, 8, LANES).transpose(0, 1, 3, 2, 4)
    return rows.reshape(shape)


def tile_order(value):
    z, x, b = value.shape
    return value.reshape(z, x // 8, 8, b).transpose(0, 1, 3, 2).reshape(z, x * b)


def iota(shape, axis):
    return lax.broadcasted_iota(jnp.int32, shape, axis)


def request_kernel(code_ref, list1_ref, list2_ref, where_ref, picked_ref):
    code = code_ref[...]
    shift = lax.shift_right_logical(code, 11)
    tile = jnp.bitwise_and(code, TILES - 1)
    before_lane = (iota((LANES, LANES), 0) < iota((LANES, LANES), 1)).astype(jnp.bfloat16)
    before_row = (iota((PLANES, PLANES), 1) < iota((PLANES, PLANES), 0)).astype(jnp.bfloat16)
    all_lanes = jnp.ones((LANES, LANES), jnp.bfloat16)
    tile_f = tile.astype(jnp.float32)
    where = tile
    for step, list_ref in ((1, list1_ref), (2, list2_ref)):
        mine = shift == step
        mask = jnp.where(mine, 1.0, 0.0).astype(jnp.bfloat16)
        inside = jnp.dot(mask, before_lane, preferred_element_type=jnp.float32)
        per_row = jnp.dot(mask, all_lanes, preferred_element_type=jnp.float32)
        ahead = jnp.dot(before_row, per_row.astype(jnp.bfloat16), preferred_element_type=jnp.float32)
        rank = (inside + ahead).astype(jnp.int32)
        where = jnp.where(mine, TILES + (step - 1) * CAP + rank, where)
        rank = jnp.where(mine, rank, -1)
        for block in range(CAP // 64):
            slot = iota((64, LANES), 0) + 64 * block
            picked = jnp.zeros((64, LANES), jnp.float32)
            for row in range(PLANES):
                picked = jnp.where(rank[row : row + 1, :] == slot, tile_f[row : row + 1, :], picked)
            picked_ref[pl.ds(64 * block, 64), :] = picked
        total = lax.dot_general(
            jnp.ones((8, LANES), jnp.float32), picked_ref[...], (((1,), (1,)), ((), ())),
            precision=HIGH, preferred_element_type=jnp.float32,
        )
        list_ref[...] = total[0:1, :].astype(jnp.int32)
    where_ref[...] = where


def request(code):
    return pl.pallas_call(
        request_kernel,
        out_shape=(
            jax.ShapeDtypeStruct((1, CAP), jnp.int32),
            jax.ShapeDtypeStruct((1, CAP), jnp.int32),
            jax.ShapeDtypeStruct((PLANES, LANES), jnp.int32),
        ),
        in_specs=[pl.BlockSpec(memory_space=VMEM)],
        out_specs=[pl.BlockSpec(memory_space=VMEM)] * 3,
        scratch_shapes=[pltpu.VMEM((CAP, LANES), jnp.float32)],
        name="request",
    )(code)


def serve_kernel(list1_ref, list2_ref, rows_ref, out1_ref, out2_ref):
    for list_ref, out_ref in ((list1_ref, out1_ref), (list2_ref, out2_ref)):

        def step(k, carry, list_ref=list_ref, out_ref=out_ref):
            for j in range(32):
                slot = k * 32 + j
                out_ref[pl.ds(slot, 1), :] = rows_ref[pl.ds(list_ref[0, slot], 1), :]
            return carry

        lax.fori_loop(0, CAP // 32, step, 0)


def serve(list1, list2, rows):
    out = jax.ShapeDtypeStruct((CAP, LANES), jnp.float32)
    return pl.pallas_call(
        serve_kernel,
        out_shape=(out, out),
        in_specs=[pl.BlockSpec(memory_space=SMEM)] * 2 + [pl.BlockSpec(memory_space=VMEM)],
        out_specs=[pl.BlockSpec(memory_space=VMEM)] * 2,
        name="serve",
    )(list1, list2, rows)


def coef_kernel(kl_ref, kr_ref, mine_ref, mats_ref, own_ref, red_ref, diag_ref, own_t, row_t):
    devices = red_ref.shape[1]
    kl, kr = kl_ref[...], kr_ref[...]
    main = 1.0 + kl + kr
    row = lambda a, z: a[z : z + 1, :]
    inv, low, up = [], [], []
    for z in range(PLANES):
        pivot = row(main, z) if z == 0 else row(main, z) - row(kr, z - 1) * low_up
        inv.append(1.0 / pivot)
        low.append(jnp.zeros_like(pivot) if z == 0 else row(kr, z - 1) * inv[z])
        up.append(row(kr, z) * inv[z])
        low_up = up[z]
    left = [row(kl, 0) * inv[0]]
    for z in range(1, PLANES):
        left.append(low[z] * left[z - 1])
    right = [None] * PLANES
    right[-1] = row(kr, PLANES - 1) * inv[-1]
    for z in range(PLANES - 2, -1, -1):
        left[z] = left[z] + up[z] * left[z + 1]
        right[z] = up[z] * right[z + 1]
    mine = mine_ref[...]
    ones = jnp.ones((LANES, LANES), jnp.float32)
    for kind, values in enumerate((inv, low, up, left, right)):
        for z in range(PLANES):
            own_t[pl.ds(kind * PLANES + z, 1), :] = jnp.where(mine > 0.0, values[z], 0.0)
    own_ref[...] = jnp.dot(own_t[...], ones, precision=HIGH, preferred_element_type=jnp.float32)
    eye = iota((devices, LANES), 0) == iota((devices, LANES), 1)
    for kind, value in enumerate((left[0], left[-1], right[0], right[-1])):
        row_t[pl.ds(kind * devices, devices), :] = jnp.where(eye, value, 0.0)
    spread = jnp.dot(row_t[...], ones, precision=HIGH, preferred_element_type=jnp.float32)
    ratio = jnp.zeros((1, LANES), jnp.float32)
    for d in range(devices):
        l_first, l_last, r_first, r_last = (row(spread, kind * devices + d) for kind in range(4))
        gain = 1.0 / (1.0 - l_first * ratio)
        for kind, value in enumerate(
            (l_last * ratio * gain, l_last * gain, gain, gain * l_first, gain * r_first, ratio)
        ):
            red_ref[kind, pl.ds(d, 1), :] = value
        ratio = r_last + l_last * ratio * gain * r_first
    r, c = iota((LANES, LANES), 0), iota((LANES, LANES), 1)
    diag_ref[...] = jnp.zeros_like(diag_ref)
    for kind, at in enumerate((r == c, r == c + 1, r == c - 1)):
        lanes = pl.ds(kind * LANES, LANES)
        values = jnp.concatenate(
            [jnp.sum(jnp.where(at, mats_ref[m], 0.0), axis=0, keepdims=True) for m in range(NMAT)], axis=0
        )
        first = values.astype(jnp.bfloat16).astype(jnp.float32)
        second = (values - first).astype(jnp.bfloat16).astype(jnp.float32)
        third = values - first - second
        stacked = jnp.concatenate([first, second, third, jnp.zeros_like(first)], axis=0)
        diag_ref[:, lanes] = stacked.astype(jnp.bfloat16)


def coefficients(kl, kr, mine, mats, devices):
    return pl.pallas_call(
        coef_kernel,
        out_shape=(
            jax.ShapeDtypeStruct((5 * PLANES, LANES), jnp.float32),
            jax.ShapeDtypeStruct((6, devices, LANES), jnp.float32),
            jax.ShapeDtypeStruct((4 * NMAT, 3 * LANES), jnp.bfloat16),
        ),
        in_specs=[pl.BlockSpec(memory_space=VMEM)] * 4,
        out_specs=[pl.BlockSpec(memory_space=VMEM)] * 3,
        scratch_shapes=[
            pltpu.VMEM((5 * PLANES, LANES), jnp.float32),
            pltpu.VMEM((4 * devices, LANES), jnp.float32),
        ],
        name="coefficients",
    )(kl, kr, mine, mats)


def slab_kernel(
    where_ref, rows_hbm, got1_hbm, got2_hbm, one_ref, two_ref, class_ref, diag_ref, own_ref,
    base_ref, ends_ref, src, dep, partial, sems,
):
    copies = [
        pltpu.make_async_copy(rows_hbm, src.at[pl.ds(0, TILES)], sems.at[0]),
        pltpu.make_async_copy(got1_hbm, src.at[pl.ds(TILES, CAP)], sems.at[1]),
        pltpu.make_async_copy(got2_hbm, src.at[pl.ds(TILES + CAP, CAP)], sems.at[2]),
    ]
    for copy in copies:
        copy.start()
    for copy in copies:
        copy.wait()
    diag = diag_ref[...]
    of_class = jnp.bitwise_and(iota((4 * NMAT, ROWS), 0), NMAT - 1)

    def own(kind, z):
        return own_ref[pl.ds(kind * PLANES + z, 1), :]

    def forward(z, before):
        for j in range(ROWS):
            dep[pl.ds(j, 1), :] = src[pl.ds(where_ref[z, j], 1), :]
        here = pl.ds(pl.multiple_of(z * ROWS, ROWS), ROWS)
        chosen = jnp.where(of_class == class_ref[pl.ds(z, 1), :], 1.0, 0.0).astype(jnp.bfloat16)
        weights = lax.dot_general(
            chosen, diag, (((0,), (0,)), ((), ())), preferred_element_type=jnp.float32
        )
        cells = dep[...]
        adv = (
            weights[:, :LANES] * cells
            + pltpu.roll(weights[:, LANES : 2 * LANES] * cells, 1, 1)
            + pltpu.roll(weights[:, 2 * LANES :] * cells, LANES - 1, 1)
        )
        a, b = 0.5 + adv, 2.0 + adv
        ab = a * b
        free = adv * ab / (ab + one_ref[here, :] * b + two_ref[here, :] * a)
        base_ref[here, :] = adv - free
        before = free * own(0, z) + before * own(1, z)
        partial[here, :] = before
        return before

    last = lax.fori_loop(0, PLANES, forward, jnp.zeros((ROWS, LANES), jnp.float32))

    def backward(k, after):
        z = PLANES - 1 - k
        here = pl.ds(pl.multiple_of(z * ROWS, ROWS), ROWS)
        after = partial[here, :] + after * own(2, z)
        base_ref[here, :] = base_ref[here, :] + after
        return after

    first = lax.fori_loop(0, PLANES, backward, jnp.zeros((ROWS, LANES), jnp.float32))
    share = ends_ref.shape[1] // 2
    for d in range(ends_ref.shape[0]):
        ends_ref[d, pl.ds(0, share), :] = first[d * share : (d + 1) * share, :]
        ends_ref[d, pl.ds(share, share), :] = last[d * share : (d + 1) * share, :]


def slab(where, rows, got1, got2, one, two, classes, diag, own, devices):
    return pl.pallas_call(
        slab_kernel,
        out_shape=(
            jax.ShapeDtypeStruct((TILES, LANES), jnp.float32),
            jax.ShapeDtypeStruct((devices, 2 * ROWS // devices, LANES), jnp.float32),
        ),
        in_specs=[pl.BlockSpec(memory_space=SMEM)]
        + [pl.BlockSpec(memory_space=pl.ANY)] * 3
        + [pl.BlockSpec(memory_space=VMEM)] * 5,
        out_specs=[pl.BlockSpec(memory_space=VMEM)] * 2,
        scratch_shapes=[
            pltpu.VMEM((TILES + 2 * CAP, LANES), jnp.float32),
            pltpu.VMEM((ROWS, LANES), jnp.float32),
            pltpu.VMEM((TILES, LANES), jnp.float32),
            pltpu.SemaphoreType.DMA((3,)),
        ],
        name="slab",
    )(where, rows, got1, got2, one, two, classes, diag, own)


def interface_kernel(ends_ref, red_ref, out_ref, carry_ref):
    devices, both, _ = ends_ref.shape
    share = both // 2
    coef = lambda kind, d: red_ref[kind, pl.ds(d, 1), :]
    upto = jnp.zeros((share, LANES), jnp.float32)
    for d in range(devices):
        first, last = ends_ref[d, pl.ds(0, share), :], ends_ref[d, pl.ds(share, share), :]
        carry_ref[d] = upto
        upto = last + coef(0, d) * first + coef(1, d) * upto
    after = jnp.zeros((share, LANES), jnp.float32)
    for d in range(devices - 1, -1, -1):
        first = ends_ref[d, pl.ds(0, share), :]
        out_ref[d, pl.ds(share, share), :] = after
        after = coef(2, d) * first + coef(3, d) * carry_ref[d] + coef(4, d) * after
        out_ref[d, pl.ds(0, share), :] = carry_ref[d] + coef(5, d) * after


def interface(ends, red):
    devices, both, _ = ends.shape
    return pl.pallas_call(
        interface_kernel,
        out_shape=jax.ShapeDtypeStruct(ends.shape, jnp.float32),
        in_specs=[pl.BlockSpec(memory_space=VMEM)] * 2,
        out_specs=pl.BlockSpec(memory_space=VMEM),
        scratch_shapes=[pltpu.VMEM((devices, both // 2, LANES), jnp.float32)],
        name="interface",
    )(ends, red)


def finish_kernel(base_ref, near_ref, own_ref, out_ref, left_t, right_t):
    devices, both, _ = near_ref.shape
    share = both // 2
    for d in range(devices):
        left_t[pl.ds(d * share, share), :] = near_ref[d, pl.ds(0, share), :]
        right_t[pl.ds(d * share, share), :] = near_ref[d, pl.ds(share, share), :]
    left, right = left_t[...], right_t[...]
    for z in range(PLANES):
        here = pl.ds(z * ROWS, ROWS)
        from_left = own_ref[pl.ds(3 * PLANES + z, 1), :]
        from_right = own_ref[pl.ds(4 * PLANES + z, 1), :]
        out_ref[here, :] = base_ref[here, :] + from_left * left + from_right * right


def finish(base, near, own):
    return pl.pallas_call(
        finish_kernel,
        out_shape=jax.ShapeDtypeStruct(base.shape, jnp.float32),
        in_specs=[pl.BlockSpec(memory_space=VMEM)] * 3,
        out_specs=pl.BlockSpec(memory_space=VMEM),
        scratch_shapes=[pltpu.VMEM((ROWS, LANES), jnp.float32)] * 2,
        name="finish",
    )(base, near, own)


def local(
    conc, target_one, target_two, diffusivity, src_shift, src_tile, interp_class, interp_mats
):
    devices = lax.axis_size("gy")
    rows = to_rows(conc)
    place = (src_tile & -64) | ((src_tile & 7) << 3) | ((src_tile >> 3) & 7)
    code = tile_order(src_shift * TILES + place)
    list1, list2, where = request(code)
    asked1, asked2 = shifted(list1, "gx", -1), shifted(list2, "gx", -2)
    face = 0.5 * (diffusivity[1:] + diffusivity[:-1])
    kl = jnp.pad(face, (1, 0)).reshape(devices, PLANES).T
    kr = jnp.pad(face, (0, 1)).reshape(devices, PLANES).T
    wide = ((0, 0), (0, LANES - devices))
    mine = (iota((1, LANES), 1) == lax.axis_index("gy")).astype(jnp.float32)
    own, red, diag = coefficients(jnp.pad(kl, wide), jnp.pad(kr, wide), mine, interp_mats, devices)
    send1, send2 = serve(asked1, asked2, rows)
    got1, got2 = shifted(send1, "gx", 1), shifted(send2, "gx", 2)
    base, ends = slab(
        where, rows, got1, got2, to_rows(target_one), to_rows(target_two),
        tile_order(interp_class), diag, own, devices,
    )
    ends = lax.all_to_all(ends, "gy", split_axis=0, concat_axis=0, tiled=True)
    near = interface(ends, red)
    near = lax.all_to_all(near, "gy", split_axis=0, concat_axis=0, tiled=True)
    return from_rows(finish(base, near, own), conc.shape)


def solution(mesh):
    slabs = P("gy", "gx", None)
    in_specs = (slabs, slabs, slabs, P(), slabs, slabs, slabs, P())
    return jax.shard_map(local, mesh=mesh, in_specs=in_specs, out_specs=slabs, check_vma=False)
```

time: 2170 us -> 106 us (0.05)
  the two profiles are of different devices: /device:TPU:10 before, /device:TPU:6 now
where the time goes in v1:
time: 106 us
  blocking collectives  54.5 us (51%)
  Pallas kernels  21.9 us (21%)
  starting transfers between devices  11.8 us (11%)
  waiting for transfers between devices  11.4 us (11%)
  local copies, waits for them, and re-layouts  5.42 us (5%)
    all_to_all x1, blocking collectives, local(): ends = lax.all_to_all(ends, 'gy', split_axis=0, concat_axis=0, tiled=True)  32.8 us
    all_to_all x1, blocking collectives, local(): near = lax.all_to_all(near, 'gy', split_axis=0, concat_axis=0, tiled=True)  21.7 us
    ppermute x4, starting transfers between devices, shifted(): return lax.ppermute(value, axis, pairs)  11.8 us
    ppermute x4, waiting for transfers between devices, shifted(): return lax.ppermute(value, axis, pairs)  11.4 us
    pallas_call x1, Pallas kernels, slab(): pl.pallas_call(slab_kernel, out_shape=(jax.ShapeDtypeStruct((TILES, LANES...  9.13 us
    pallas_call x1, Pallas kernels, serve(): pl.pallas_call(serve_kernel, out_shape=(out, out), in_specs=[pl.BlockSpec...  2.98 us
    pallas_call x1, Pallas kernels, request(): pl.pallas_call(request_kernel, out_shape=(jax.ShapeDtypeStruct((1, CAP),...  2.96 us
    pallas_call x1, Pallas kernels, coefficients(): pl.pallas_call(coef_kernel, out_shape=(jax.ShapeDtypeStruct((5 * PLANES,...  2.59 us
  transfers between devices with their start and end apart: 4, of which 3 were waited for; matrix products, arithmetic and copies ran while one was open for 3% of the time, Pallas kernels for 2%

profile of v1, /device:TPU:6, one launch (start us, length us, event | category | flops | bytes accessed | tf_op | source)
XLA Modules:
  0.0 105.8 jit_solution(14644683362139448570)
XLA Ops:
  0.0 1.0 copy.11
  1.0 0.1 copy.12
  1.1 0.7 copy.16.code_ref
  1.8 3.0 %request.1 = (s32[1,512]{1,0:T(1,128)}, s32[1,512]{1,0:T(1,128)}, s32[16,128]{1,0:T(8,128)}) custom-call(s32[16,128]{1,0:T(8,128)} %copy.16.code_ref), custom_call_target="tpu_custom_call" | custom-call | tf_op jit(solution)/shard_map/request/pallas_call | solution.py:81
  4.8 5.3 %collective-permute-start = (s32[1,512]{1,0:T(1,128)}, s32[1,512]{1,0:T(1,128)S(1)}, u32[]{:S(2)}, u32[]{:S(2)}) collective-permute-start(s32[1,512]{1,0:T(1,128)} %get-tuple-element.16), channel_id=1, source_target_pairs={{32,0},{64,32},{96,64},{128,96},{160,128},{192,160},{224,192},{256... | collective-permute-start | bytes 6152 | tf_op jit(solution)/shard_map/ppermute | solution.py:24
  10.1 2.5 %collective-permute-start.1 = (s32[1,512]{1,0:T(1,128)S(1)}, s32[1,512]{1,0:T(1,128)S(1)}, u32[]{:S(2)}, u32[]{:S(2)}) collective-permute-start(s32[1,512]{1,0:T(1,128)S(1)} %copy-done.7), channel_id=1, source_target_pairs={{64,0},{96,32},{128,64},{160,96},{192,128},{224,160},{256,192},{28... | collective-permute-start | bytes 6152 | tf_op jit(solution)/shard_map/ppermute | solution.py:24
  12.7 4.4 %collective-permute-done.1.list2_ref = s32[1,512]{1,0:T(1,128)S(1)} collective-permute-done((s32[1,512]{1,0:T(1,128)S(1)}, s32[1,512]{1,0:T(1,128)S(1)}, u32[]{:S(2)}, u32[]{:S(2)}) %collective-permute-start.1) | collective-permute-done | bytes 2080 | tf_op jit(solution)/shard_map/ppermute | solution.py:24
  17.1 0.6 copy-done.6
  17.7 3.0 %serve.1 = (f32[512,128]{1,0:T(8,128)}, f32[512,128]{1,0:T(8,128)}) custom-call(s32[1,512]{1,0:T(1,128)} %copy-done.5, s32[1,512]{1,0:T(1,128)} %copy-done.6, f32[2048,128]{1,0:T(8,128)} %bitcast.30), custom_call_target="tpu_custom_call" | custom-call | tf_op jit(solution)/shard_map/serve/pallas_call | solution.py:109
  20.6 2.0 %collective-permute-start.2 = (f32[512,128]{1,0:T(8,128)}, f32[512,128]{1,0:T(8,128)S(1)}, u32[]{:S(2)}, u32[]{:S(2)}) collective-permute-start(f32[512,128]{1,0:T(8,128)} %get-tuple-element.18), channel_id=1, source_target_pairs={{0,32},{32,64},{64,96},{96,128},{128,160},{160,192},{192,224},{224... | collective-permute-start | bytes 786440 | tf_op jit(solution)/shard_map/ppermute | solution.py:24
  22.7 1.9 %collective-permute-start.3 = (f32[512,128]{1,0:T(8,128)}, f32[512,128]{1,0:T(8,128)S(1)}, u32[]{:S(2)}, u32[]{:S(2)}) collective-permute-start(f32[512,128]{1,0:T(8,128)} %get-tuple-element.19), channel_id=1, source_target_pairs={{0,64},{32,96},{64,128},{96,160},{128,192},{160,224},{192,256},{22... | collective-permute-start | bytes 786440 | tf_op jit(solution)/shard_map/ppermute | solution.py:24
  25.1 0.6 pad.18.kr_ref
  25.7 0.6 pad.16.kl_ref
  26.4 0.7 copy.21.class_ref
  27.1 0.5 compare_convert_fusion.mine_ref
  27.6 2.6 %coefficients.1 = (f32[80,128]{1,0:T(8,128)}, f32[6,32,128]{2,1,0:T(8,128)}, bf16[32,384]{1,0:T(8,128)(2,1)}) custom-call(f32[16,128]{1,0:T(8,128)} %pad.16.kl_ref, f32[16,128]{1,0:T(8,128)} %pad.18.kr_ref, f32[1,128]{1,0:T(1,128)} %compare_convert_fusion.mine_ref, f32[8,128,128]{2,1,0:T(8,128)} %mats_ref.1), custom_call_target="tpu_custom_call" | custom-call | tf_op jit(solution)/shard_map/coefficients/pallas_call | solution.py:172
  30.2 5.6 %collective-permute-done.2.got1_hbm = f32[512,128]{1,0:T(8,128)S(1)} collective-permute-done((f32[512,128]{1,0:T(8,128)}, f32[512,128]{1,0:T(8,128)S(1)}, u32[]{:S(2)}, u32[]{:S(2)}) %collective-permute-start.2) | collective-permute-done | bytes 262176 | tf_op jit(solution)/shard_map/ppermute | solution.py:24
  35.8 1.4 %collective-permute-done.3.got2_hbm = f32[512,128]{1,0:T(8,128)S(1)} collective-permute-done((f32[512,128]{1,0:T(8,128)}, f32[512,128]{1,0:T(8,128)S(1)}, u32[]{:S(2)}, u32[]{:S(2)}) %collective-permute-start.3) | collective-permute-done | bytes 262176 | tf_op jit(solution)/shard_map/ppermute | solution.py:24
  37.2 0.7 copy-done.1
  37.9 9.1 %slab.1 = (f32[2048,128]{1,0:T(8,128)}, f32[32,8,128]{2,1,0:T(8,128)}) custom-call(s32[16,128]{1,0:T(8,128)} %get-tuple-element.15.where_ref, f32[2048,128]{1,0:T(8,128)} %bitcast.31, f32[512,128]{1,0:T(8,128)} %copy-done, f32[512,128]{1,0:T(8,128)} %copy-done.1, f32[2048,128]{1,0:T(8,128)} %bitcast.32, f32[2048,128]{1,0:T(8,128)} %bitcast.33, ...), custom_call_target="tpu_custom_call" | custom-call | tf_op jit(solution)/shard_map/slab/pallas_call | solution.py:247
  47.1 32.8 %all_to_all.10.ends_ref = f32[32,8,128]{2,1,0:T(8,128)} all-to-all(f32[32,8,128]{2,1,0:T(8,128)} %get-tuple-element.23), channel_id=1, replica_groups=mesh['gx'=16,'gy'=32] {'gy'}, dimensions={0} | all-to-all | bytes 262144 | tf_op jit(solution)/shard_map/all_to_all | solution.py:342
  79.9 1.8 %interface.1 = f32[32,8,128]{2,1,0:T(8,128)} custom-call(f32[32,8,128]{2,1,0:T(8,128)} %all_to_all.10.ends_ref, f32[6,32,128]{2,1,0:T(8,128)} %get-tuple-element.24.red_ref), custom_call_target="tpu_custom_call" | custom-call | tf_op jit(solution)/shard_map/interface/pallas_call | solution.py:286
  81.6 21.7 %all_to_all.11.near_ref = f32[32,8,128]{2,1,0:T(8,128)} all-to-all(f32[32,8,128]{2,1,0:T(8,128)} %interface.1), channel_id=1, replica_groups=mesh['gx'=16,'gy'=32] {'gy'}, dimensions={0} | all-to-all | bytes 262144 | tf_op jit(solution)/shard_map/all_to_all | solution.py:344
  103.4 2.5 %finish.1 = f32[2048,128]{1,0:T(8,128)} custom-call(f32[2048,128]{1,0:T(8,128)} %get-tuple-element.22.base_ref, f32[32,8,128]{2,1,0:T(8,128)} %all_to_all.11.near_ref, f32[80,128]{1,0:T(8,128)} %get-tuple-element.21.own_ref), custom_call_target="tpu_custom_call" | custom-call | tf_op jit(solution)/shard_map/finish/pallas_call | solution.py:311
  (25 shorter events, 0.6 us)
Async XLA Ops:
  0.0 1.0 copy-start.2
  4.8 5.3 %copy-start.7 = (s32[1,512]{1,0:T(1,128)S(1)}, s32[1,512]{1,0:T(1,128)}, u32[]{:S(2)}) copy-start(s32[1,512]{1,0:T(1,128)} %get-tuple-element.17) | copy-start | bytes 6148
  4.8 7.9 %collective-permute-start = (s32[1,512]{1,0:T(1,128)}, s32[1,512]{1,0:T(1,128)S(1)}, u32[]{:S(2)}, u32[]{:S(2)}) collective-permute-start(s32[1,512]{1,0:T(1,128)} %get-tuple-element.16), channel_id=1, source_target_pairs={{32,0},{64,32},{96,64},{128,96},{160,128},{192,160},{224,192},{256... | collective-permute-start | bytes 6152 | tf_op jit(solution)/shard_map/ppermute | solution.py:24
  10.1 7.0 %collective-permute-start.1 = (s32[1,512]{1,0:T(1,128)S(1)}, s32[1,512]{1,0:T(1,128)S(1)}, u32[]{:S(2)}, u32[]{:S(2)}) collective-permute-start(s32[1,512]{1,0:T(1,128)S(1)} %copy-done.7), channel_id=1, source_target_pairs={{64,0},{96,32},{128,64},{160,96},{192,128},{224,160},{256,192},{28... | collective-permute-start | bytes 6152 | tf_op jit(solution)/shard_map/ppermute | solution.py:24
  12.6 4.4 %copy-start.5 = (s32[1,512]{1,0:T(1,128)}, s32[1,512]{1,0:T(1,128)S(1)}, u32[]{:S(2)}) copy-start(s32[1,512]{1,0:T(1,128)S(1)} %collective-permute-done.list1_ref) | copy-start | bytes 6148
  17.1 0.6 copy-start.6
  20.6 4.0 %copy-start.4 = (f32[512]{0:T(512)S(1)}, f32[512]{0:T(512)}, u32[]{:S(2)}) copy-start(f32[512]{0:T(512)} %param.11) | copy-start | bytes 6148
  20.6 15.1 %collective-permute-start.2 = (f32[512,128]{1,0:T(8,128)}, f32[512,128]{1,0:T(8,128)S(1)}, u32[]{:S(2)}, u32[]{:S(2)}) collective-permute-start(f32[512,128]{1,0:T(8,128)} %get-tuple-element.18), channel_id=1, source_target_pairs={{0,32},{32,64},{64,96},{96,128},{128,160},{160,192},{192,224},{224... | collective-permute-start | bytes 786440 | tf_op jit(solution)/shard_map/ppermute | solution.py:24
  22.7 14.5 %collective-permute-start.3 = (f32[512,128]{1,0:T(8,128)}, f32[512,128]{1,0:T(8,128)S(1)}, u32[]{:S(2)}, u32[]{:S(2)}) collective-permute-start(f32[512,128]{1,0:T(8,128)} %get-tuple-element.19), channel_id=1, source_target_pairs={{0,64},{32,96},{64,128},{96,160},{128,192},{160,224},{192,256},{22... | collective-permute-start | bytes 786440 | tf_op jit(solution)/shard_map/ppermute | solution.py:24
  24.7 1.6 %copy-start.3 = (s32[16,16,8]{1,2,0:T(8,128)S(1)}, s32[16,16,8]{1,2,0:T(8,128)}, u32[]{:S(2)}) copy-start(s32[16,16,8]{1,2,0:T(8,128)} %param.14) | copy-start | bytes 24580
  35.8 1.4 %copy-start = (f32[512,128]{1,0:T(8,128)}, f32[512,128]{1,0:T(8,128)S(1)}, u32[]{:S(2)}) copy-start(f32[512,128]{1,0:T(8,128)S(1)} %collective-permute-done.2.got1_hbm) | copy-start | bytes 786436
  37.2 0.7 copy-start.1

commit v2 on v1

v2 whole, which is shorter than its diff:
```python
import jax
import jax.numpy as jnp
from jax import lax
from jax.experimental import pallas as pl
from jax.experimental.pallas import tpu as pltpu
from jax.sharding import PartitionSpec as P

LANES = 128
NMAT = 8
PLANES = 16
ROWS = 128
TILES = PLANES * ROWS
CAP = 512
HIGH = lax.Precision.HIGHEST
VMEM = pl.BlockSpec(memory_space=pltpu.VMEM)
SMEM = pl.BlockSpec(memory_space=pltpu.SMEM)
PARAMS = pltpu.CompilerParams(vmem_limit_bytes=24 << 20)


def near(value):
    return pltpu.with_memory_space_constraint(value, pltpu.VMEM)


def shifted(value, axis, by):
    peers = lax.axis_size(axis)
    pairs = [(i, i + by) for i in range(peers) if 0 <= i + by < peers]
    return lax.ppermute(value, axis, pairs)


def to_rows(value):
    z, x, y = value.shape
    value = value.reshape(z, x // 8, 8, y // LANES, LANES).transpose(0, 1, 3, 2, 4)
    return value.reshape(z * x * (y // LANES), LANES)


def from_rows(rows, shape):
    z, x, y = shape
    rows = rows.reshape(z, x // 8, y // LANES, 8, LANES).transpose(0, 1, 3, 2, 4)
    return rows.reshape(shape)


def iota(shape, axis):
    return lax.broadcasted_iota(jnp.int32, shape, axis)


def by_lanes(ref):
    return jnp.concatenate([ref[:, b, :] for b in range(ref.shape[1])], axis=1)


def ranks_of(mine):
    before_lane = (iota((LANES, LANES), 0) < iota((LANES, LANES), 1)).astype(jnp.bfloat16)
    before_row = (iota((PLANES, PLANES), 1) < iota((PLANES, PLANES), 0)).astype(jnp.bfloat16)
    all_lanes = jnp.ones((LANES, LANES), jnp.bfloat16)
    mask = jnp.where(mine, 1.0, 0.0).astype(jnp.bfloat16)
    inside = jnp.dot(mask, before_lane, preferred_element_type=jnp.float32)
    per_row = jnp.dot(mask, all_lanes, preferred_element_type=jnp.float32)
    ahead = jnp.dot(before_row, per_row.astype(jnp.bfloat16), preferred_element_type=jnp.float32)
    return jnp.where(mine, (inside + ahead).astype(jnp.int32), -1)


def compact(rank, value, empty, picked_ref):
    for block in range(CAP // 64):
        slot = iota((64, LANES), 0) + 64 * block
        picked = jnp.zeros((64, LANES), jnp.float32)
        for row in range(PLANES):
            picked = jnp.where(rank[row : row + 1, :] == slot, value[row : row + 1, :] - empty, picked)
        picked_ref[pl.ds(64 * block, 64), :] = picked
    total = lax.dot_general(
        jnp.ones((8, LANES), jnp.float32), picked_ref[...], (((1,), (1,)), ((), ())),
        precision=HIGH, preferred_element_type=jnp.float32,
    )
    return (total[0:1, :] + empty).astype(jnp.int32)


def request_kernel(shift_ref, tile_ref, list1_ref, list2_ref, place_ref, shift_out, picked_ref):
    shift, tile = by_lanes(shift_ref), by_lanes(tile_ref)
    place = (tile & -64) | ((tile & 7) << 3) | (lax.shift_right_logical(tile, 3) & 7)
    place_ref[...] = place
    shift_out[...] = shift
    place = place.astype(jnp.float32)
    for step, list_ref in ((1, list1_ref), (2, list2_ref)):
        list_ref[...] = compact(ranks_of(shift == step), place, 0.0, picked_ref)


def request(shift, tile):
    return pl.pallas_call(
        request_kernel,
        out_shape=(
            pltpu.VMEM((1, CAP), jnp.int32),
            pltpu.VMEM((1, CAP), jnp.int32),
            jax.ShapeDtypeStruct((PLANES, LANES), jnp.int32),
            pltpu.VMEM((PLANES, LANES), jnp.int32),
        ),
        in_specs=[VMEM] * 2,
        out_specs=[VMEM] * 4,
        scratch_shapes=[pltpu.VMEM((CAP, LANES), jnp.float32)],
        compiler_params=PARAMS,
        name="request",
    )(near(shift), near(tile))


def serve_kernel(list1_ref, list2_ref, rows_ref, out1_ref, out2_ref):
    for list_ref, out_ref in ((list1_ref, out1_ref), (list2_ref, out2_ref)):

        def step(k, carry, list_ref=list_ref, out_ref=out_ref):
            for j in range(32):
                slot = k * 32 + j
                out_ref[pl.ds(slot, 1), :] = rows_ref[pl.ds(list_ref[0, slot], 1), :]
            return carry

        lax.fori_loop(0, CAP // 32, step, 0)


def serve(list1, list2, rows):
    out = pltpu.VMEM((CAP, LANES), jnp.float32)
    return pl.pallas_call(
        serve_kernel,
        out_shape=(out, out),
        in_specs=[SMEM] * 2 + [VMEM],
        out_specs=[VMEM] * 2,
        compiler_params=PARAMS,
        name="serve",
    )(list1, list2, rows)


def coef_kernel(diff_ref, mats_ref, own_ref, red_ref, diag_ref, own_t, row_t):
    devices = red_ref.shape[1]
    row = lambda a, z: a[z : z + 1, :]
    lane = iota((1, LANES), 1)
    plane_of = (iota((PLANES, LANES), 1) & (PLANES - 1)) == iota((PLANES, LANES), 0)
    diff = jnp.zeros((PLANES, LANES), jnp.float32)
    per_row = LANES // PLANES
    for r in range(diff_ref.shape[0]):
        goes = iota((LANES, LANES), 1) == lax.shift_right_logical(iota((LANES, LANES), 0), 4) + per_row * r
        diff = diff + jnp.dot(
            jnp.where(plane_of, diff_ref[pl.ds(r, 1), :], 0.0), jnp.where(goes, 1.0, 0.0),
            precision=HIGH, preferred_element_type=jnp.float32,
        )
    kr = [0.5 * (row(diff, z + 1) + row(diff, z)) for z in range(PLANES - 1)]
    beyond = pltpu.roll(diff, LANES - 1, 1)
    kr.append(jnp.where(lane < devices - 1, 0.5 * (row(beyond, 0) + row(diff, PLANES - 1)), 0.0))
    kl = [jnp.where(lane > 0, pltpu.roll(jnp.broadcast_to(kr[-1], (8, LANES)), 1, 1)[0:1, :], 0.0)]
    kl = kl + kr[:-1]
    inv, low, up = [], [], []
    for z in range(PLANES):
        pivot = 1.0 + kl[z] + kr[z]
        if z > 0:
            pivot = pivot - kr[z - 1] * up[z - 1]
        inv.append(1.0 / pivot)
        low.append(jnp.zeros_like(pivot) if z == 0 else kr[z - 1] * inv[z])
        up.append(kr[z] * inv[z])
    left = [kl[0] * inv[0]]
    for z in range(1, PLANES):
        left.append(low[z] * left[z - 1])
    right = [None] * PLANES
    right[-1] = up[-1]
    for z in range(PLANES - 2, -1, -1):
        left[z] = left[z] + up[z] * left[z + 1]
        right[z] = up[z] * right[z + 1]
    mine = lane == lax.axis_index("gy")
    ones = jnp.ones((LANES, LANES), jnp.float32)
    for kind, values in enumerate((inv, low, up, left, right)):
        for z in range(PLANES):
            own_t[pl.ds(kind * PLANES + z, 1), :] = jnp.where(mine, values[z], 0.0)
    own_ref[...] = jnp.dot(own_t[...], ones, precision=HIGH, preferred_element_type=jnp.float32)
    eye = iota((devices, LANES), 0) == iota((devices, LANES), 1)
    for kind, value in enumerate((left[0], left[-1], right[0], right[-1])):
        row_t[pl.ds(kind * devices, devices), :] = jnp.where(eye, value, 0.0)
    spread = jnp.dot(row_t[...], ones, precision=HIGH, preferred_element_type=jnp.float32)
    ratio = jnp.zeros((1, LANES), jnp.float32)
    for d in range(devices):
        l_first, l_last, r_first, r_last = (row(spread, kind * devices + d) for kind in range(4))
        gain = 1.0 / (1.0 - l_first * ratio)
        for kind, value in enumerate(
            (l_last * ratio * gain, l_last * gain, gain, gain * l_first, gain * r_first, ratio)
        ):
            red_ref[kind, pl.ds(d, 1), :] = value
        ratio = r_last + l_last * ratio * gain * r_first
    r, c = iota((LANES, LANES), 0), iota((LANES, LANES), 1)
    for kind, at in enumerate((r == c, r == c + 1, r == c - 1)):
        values = jnp.concatenate(
            [jnp.sum(jnp.where(at, mats_ref[m], 0.0), axis=0, keepdims=True) for m in range(NMAT)], axis=0
        )
        first = values.astype(jnp.bfloat16).astype(jnp.float32)
        second = (values - first).astype(jnp.bfloat16).astype(jnp.float32)
        third = values - first - second
        stacked = jnp.concatenate([first, second, third, jnp.zeros_like(first)], axis=0)
        diag_ref[:, pl.ds(kind * LANES, LANES)] = stacked.astype(jnp.bfloat16)


def coefficients(diffusivity, mats, devices):
    return pl.pallas_call(
        coef_kernel,
        out_shape=(
            pltpu.VMEM((5 * PLANES, LANES), jnp.float32),
            pltpu.VMEM((6, devices, LANES), jnp.float32),
            pltpu.VMEM((4 * NMAT, 3 * LANES), jnp.bfloat16),
        ),
        in_specs=[VMEM] * 2,
        out_specs=[VMEM] * 3,
        scratch_shapes=[
            pltpu.VMEM((5 * PLANES, LANES), jnp.float32),
            pltpu.VMEM((4 * devices, LANES), jnp.float32),
        ],
        compiler_params=PARAMS,
        cost_estimate=pl.CostEstimate(flops=8_000_000, bytes_accessed=4_000_000, transcendentals=0),
        name="coefficients",
    )(diffusivity.reshape(-1, LANES), near(mats))


def local_kernel(
    place_ref, rows_ref, shift_ref, class_ref, diag_ref, dep_ref, weights_ref, to1_ref, to2_ref, picked_ref
):
    shift = shift_ref[...]
    spot = iota((PLANES, LANES), 1)
    spot = ((spot & 8) << 3) | (lax.shift_right_logical(spot, 4) << 3) | (spot & 7)
    spot = (spot + ROWS * iota((PLANES, LANES), 0)).astype(jnp.float32)
    for step, to_ref in ((1, to1_ref), (2, to2_ref)):
        to_ref[...] = compact(ranks_of(shift == step), spot, float(TILES), picked_ref)
    classes = by_lanes(class_ref)
    diag = diag_ref[...]
    of_class = jnp.bitwise_and(iota((4 * NMAT, ROWS), 0), NMAT - 1)
    for z in range(PLANES):
        chosen = jnp.where(of_class == classes[z : z + 1, :], 1.0, 0.0).astype(jnp.bfloat16)
        weights = lax.dot_general(
            chosen, diag, (((0,), (0,)), ((), ())), preferred_element_type=jnp.float32
        )
        for group in range(ROWS // 8):
            at = z * ROWS + (group % 2) * 64 + (group // 2) * 8
            weights_ref[pl.ds(at, 8), :] = weights[group * 8 : group * 8 + 8, :]

    def plane(z, carry):
        start = pl.multiple_of(z * ROWS, ROWS)
        for j in range(ROWS):
            at = ((j >> 3) & 1) * 64 + (j >> 4) * 8 + (j & 7)
            dep_ref[pl.ds(start + at, 1), :] = rows_ref[pl.ds(place_ref[z, j], 1), :]
        return carry

    lax.fori_loop(0, PLANES, plane, 0)


def before_arrival(place, rows, shift, classes, diag):
    return pl.pallas_call(
        local_kernel,
        out_shape=(
            pltpu.VMEM((TILES + 8, LANES), jnp.float32),
            pltpu.VMEM((TILES, 3 * LANES), jnp.float32),
            jax.ShapeDtypeStruct((1, CAP), jnp.int32),
            jax.ShapeDtypeStruct((1, CAP), jnp.int32),
        ),
        in_specs=[SMEM] + [VMEM] * 4,
        out_specs=[VMEM] * 4,
        scratch_shapes=[pltpu.VMEM((CAP, LANES), jnp.float32)],
        compiler_params=PARAMS,
        cost_estimate=pl.CostEstimate(flops=20_000_000, bytes_accessed=10_000_000, transcendentals=0),
        name="before_arrival",
    )(place, rows, near(shift), near(classes), near(diag))


def slab_kernel(
    to1_ref, to2_ref, got1_ref, got2_ref, dep_in, weights_ref, one_ref, two_ref, own_ref,
    base_ref, ends_ref, dep_ref, partial,
):
    del dep_in
    for to_ref, got_ref in ((to1_ref, got1_ref), (to2_ref, got2_ref)):

        def patch(k, carry, to_ref=to_ref, got_ref=got_ref):
            start = pl.multiple_of(k * 32, 32)
            for j in range(32):
                dep_ref[pl.ds(to_ref[0, start + j], 1), :] = got_ref[pl.ds(start + j, 1), :]
            return carry

        lax.fori_loop(0, CAP // 32, patch, 0)

    def own(kind, z):
        return own_ref[pl.ds(kind * PLANES + z, 1), :]

    def forward(z, before):
        here = pl.ds(pl.multiple_of(z * ROWS, ROWS), ROWS)
        cells = dep_ref[here, :]
        adv = (
            weights_ref[here, pl.ds(0, LANES)] * cells
            + pltpu.roll(weights_ref[here, pl.ds(LANES, LANES)] * cells, 1, 1)
            + pltpu.roll(weights_ref[here, pl.ds(2 * LANES, LANES)] * cells, LANES - 1, 1)
        )
        a, b = 0.5 + adv, 2.0 + adv
        ab = a * b
        free = adv * ab / (ab + one_ref[here, :] * b + two_ref[here, :] * a)
        base_ref[here, :] = adv - free
        before = free * own(0, z) + before * own(1, z)
        partial[here, :] = before
        return before

    last = lax.fori_loop(0, PLANES, forward, jnp.zeros((ROWS, LANES), jnp.float32))

    def backward(k, after):
        z = PLANES - 1 - k
        here = pl.ds(pl.multiple_of(z * ROWS, ROWS), ROWS)
        after = partial[here, :] + after * own(2, z)
        base_ref[here, :] = base_ref[here, :] + after
        return after

    first = lax.fori_loop(0, PLANES, backward, jnp.zeros((ROWS, LANES), jnp.float32))
    share = ends_ref.shape[1] // 2
    for d in range(ends_ref.shape[0]):
        ends_ref[d, pl.ds(0, share), :] = first[d * share : (d + 1) * share, :]
        ends_ref[d, pl.ds(share, share), :] = last[d * share : (d + 1) * share, :]


def slab(to1, to2, got1, got2, dep, weights, one, two, own, devices):
    base, ends, _ = pl.pallas_call(
        slab_kernel,
        out_shape=(
            pltpu.VMEM((TILES, LANES), jnp.float32),
            pltpu.VMEM((devices, 2 * ROWS // devices, LANES), jnp.float32),
            pltpu.VMEM((TILES + 8, LANES), jnp.float32),
        ),
        in_specs=[SMEM] * 2 + [VMEM] * 7,
        out_specs=[VMEM] * 3,
        scratch_shapes=[pltpu.VMEM((TILES, LANES), jnp.float32)],
        input_output_aliases={4: 2},
        compiler_params=PARAMS,
        name="slab",
    )(to1, to2, near(got1), near(got2), near(dep), near(weights), near(one), near(two), near(own))
    return base, ends


def interface_kernel(ends_ref, red_ref, out_ref, carry_ref):
    devices, both, _ = ends_ref.shape
    share = both // 2
    coef = lambda kind, d: red_ref[kind, pl.ds(d, 1), :]
    upto = jnp.zeros((share, LANES), jnp.float32)
    for d in range(devices):
        first, last = ends_ref[d, pl.ds(0, share), :], ends_ref[d, pl.ds(share, share), :]
        carry_ref[d] = upto
        upto = last + coef(0, d) * first + coef(1, d) * upto
    after = jnp.zeros((share, LANES), jnp.float32)
    for d in range(devices - 1, -1, -1):
        first = ends_ref[d, pl.ds(0, share), :]
        out_ref[d, pl.ds(share, share), :] = after
        after = coef(2, d) * first + coef(3, d) * carry_ref[d] + coef(4, d) * after
        out_ref[d, pl.ds(0, share), :] = carry_ref[d] + coef(5, d) * after


def interface(ends, red):
    devices, both, _ = ends.shape
    return pl.pallas_call(
        interface_kernel,
        out_shape=pltpu.VMEM(ends.shape, jnp.float32),
        in_specs=[VMEM] * 2,
        out_specs=VMEM,
        scratch_shapes=[pltpu.VMEM((devices, both // 2, LANES), jnp.float32)],
        compiler_params=PARAMS,
        name="interface",
    )(near(ends), near(red))


def finish_kernel(base_ref, near_ref, own_ref, out_ref, left_t, right_t):
    devices, both, _ = near_ref.shape
    share = both // 2
    for d in range(devices):
        left_t[pl.ds(d * share, share), :] = near_ref[d, pl.ds(0, share), :]
        right_t[pl.ds(d * share, share), :] = near_ref[d, pl.ds(share, share), :]
    left, right = left_t[...], right_t[...]
    for z in range(PLANES):
        here = pl.ds(z * ROWS, ROWS)
        from_left = own_ref[pl.ds(3 * PLANES + z, 1), :]
        from_right = own_ref[pl.ds(4 * PLANES + z, 1), :]
        out_ref[here, :] = base_ref[here, :] + from_left * left + from_right * right


def finish(base, sides, own):
    return pl.pallas_call(
        finish_kernel,
        out_shape=jax.ShapeDtypeStruct(base.shape, jnp.float32),
        in_specs=[VMEM] * 3,
        out_specs=VMEM,
        scratch_shapes=[pltpu.VMEM((ROWS, LANES), jnp.float32)] * 2,
        compiler_params=PARAMS,
        name="finish",
    )(near(base), near(sides), near(own))


def local(
    conc, target_one, target_two, diffusivity, src_shift, src_tile, interp_class, interp_mats
):
    devices = lax.axis_size("gy")
    rows = near(to_rows(conc))
    as_stored = lambda value: value.transpose(0, 2, 1)
    list1, list2, place, shift = request(as_stored(src_shift), as_stored(src_tile))
    asked1, asked2 = shifted(list1, "gx", -1), shifted(list2, "gx", -2)
    own, red, diag = coefficients(diffusivity, interp_mats, devices)
    send1, send2 = serve(asked1, asked2, rows)
    got1, got2 = shifted(send1, "gx", 1), shifted(send2, "gx", 2)
    dep, weights, to1, to2 = before_arrival(place, rows, shift, as_stored(interp_class), diag)
    base, ends = slab(
        to1, to2, got1, got2, dep, weights, to_rows(target_one), to_rows(target_two), own, devices
    )
    ends = lax.all_to_all(ends, "gy", split_axis=0, concat_axis=0, tiled=True)
    sides = interface(ends, red)
    sides = lax.all_to_all(sides, "gy", split_axis=0, concat_axis=0, tiled=True)
    return from_rows(finish(base, sides, own), conc.shape)


def solution(mesh):
    slabs = P("gy", "gx", None)
    in_specs = (slabs, slabs, slabs, P(), slabs, slabs, slabs, P())
    return jax.shard_map(local, mesh=mesh, in_specs=in_specs, out_specs=slabs, check_vma=False)
```

time: 106 us -> 94.3 us (0.89)
  Pallas kernels: 21.9 us -> 14.4 us
  blocking collectives: 54.5 us -> 52.6 us
  waiting for transfers between devices: 11.4 us -> 9.74 us
    pallas_call x5 -> x6, Pallas kernels: 19.4 us -> 13.3 us  [the longest x1 4.44 us: before_arrival(): pl.pallas_call(local_kernel, out_shape=(pltpu.VMEM((TILES + 8, LANES), jn...]
    unnamed x19 -> x18, local copies, waits for them, and re-layouts: 2.47 us -> 5.21 us
    ppermute x4, waiting for transfers between devices: 11.4 us -> 9.74 us  [shifted(): return lax.ppermute(value, axis, pairs)]
    reshape x6 -> x0, local copies, waits for them, and re-layouts: 1.63 us -> none  [the longest x2 1.33 us: tile_order(): value.reshape(z, x // 8, 8, b).transpose(0, 1, 3, 2).reshape(z, x * b)]
    all_to_all x1, blocking collectives: 21.7 us -> 20.2 us  [local(): sides = lax.all_to_all(sides, 'gy', split_axis=0, concat_axis=0, tiled=True)]
    pad x3 -> x0, local copies, waits for them, and re-layouts: 1.29 us -> none  [the longest x1 0.62 us: local(): jnp.pad(kr, wide)]
    pallas_call x1, Pallas kernels: 2.45 us -> 1.17 us  [finish(): pl.pallas_call(finish_kernel, out_shape=jax.ShapeDtypeStruct(base.shape,...]
  transfers between devices with their start and end apart: 4 -> 4, of which waited for: 3 -> 3; matrix products, arithmetic and copies ran while one was open for 3% -> 0% of each run, Pallas kernels for 2% -> 6%
where the time goes in v2:
time: 94.3 us; the launch traced here: 93.9 us
  blocking collectives  52.6 us (56%)
  Pallas kernels  14.4 us (15%)
  starting transfers between devices  11.7 us (12%)
  waiting for transfers between devices  9.74 us (10%)
  local copies, waits for them, and re-layouts  5.21 us (6%)
    all_to_all x1, blocking collectives, local(): ends = lax.all_to_all(ends, 'gy', split_axis=0, concat_axis=0, tiled=True)  32.5 us
    all_to_all x1, blocking collectives, local(): sides = lax.all_to_all(sides, 'gy', split_axis=0, concat_axis=0, tiled=True)  20.2 us
    ppermute x4, starting transfers between devices, shifted(): return lax.ppermute(value, axis, pairs)  11.7 us
    ppermute x4, waiting for transfers between devices, shifted(): return lax.ppermute(value, axis, pairs)  9.74 us
    unnamed x18, local copies, waits for them, and re-layouts  5.21 us
    pallas_call x1, Pallas kernels, before_arrival(): pl.pallas_call(local_kernel, out_shape=(pltpu.VMEM((TILES + 8, LANES), jn...  4.44 us
    pallas_call x1, Pallas kernels, slab(): pl.pallas_call(slab_kernel, out_shape=(pltpu.VMEM((TILES, LANES), jnp.flo...  3.85 us
  transfers between devices with their start and end apart: 4, of which 3 were waited for; matrix products, arithmetic and copies ran while one was open for 0% of the time, Pallas kernels for 6%

profile of v2, /device:TPU:6, one launch (start us, length us, event | category | flops | bytes accessed | tf_op | source)
XLA Modules:
  0.0 93.9 jit_solution(2931401410676444262)
XLA Ops:
  0.0 0.9 copy-done.6
  0.9 0.8 copy-done.7
  1.7 1.7 %request.1 = (s32[1,512]{1,0:T(1,128)S(1)}, s32[1,512]{1,0:T(1,128)S(1)}, s32[16,128]{1,0:T(8,128)S(1)}, s32[16,128]{1,0:T(8,128)S(1)}) custom-call(s32[16,8,16]{2,1,0:T(8,128)S(1)} %bitcast.29, s32[16,8,16]{2,1,0:T(8,128)S(1)} %bitcast.30), custom_call_target="tpu_custom_call" | custom-call | tf_op jit(solution)/shard_map/request/pallas_call | solution.py:86
  3.5 5.2 %collective-permute-start = (s32[1,512]{1,0:T(1,128)S(1)}, s32[1,512]{1,0:T(1,128)S(1)}, u32[]{:S(2)}, u32[]{:S(2)}) collective-permute-start(s32[1,512]{1,0:T(1,128)S(1)} %get-tuple-element.25), channel_id=1, source_target_pairs={{32,0},{64,32},{96,64},{128,96},{160,128},{192,160},{224,192},{256... | collective-permute-start | bytes 6152 | tf_op jit(solution)/shard_map/ppermute | solution.py:27
  8.7 2.5 %collective-permute-start.1 = (s32[1,512]{1,0:T(1,128)S(1)}, s32[1,512]{1,0:T(1,128)S(1)}, u32[]{:S(2)}, u32[]{:S(2)}) collective-permute-start(s32[1,512]{1,0:T(1,128)S(1)} %get-tuple-element.26), channel_id=1, source_target_pairs={{64,0},{96,32},{128,64},{160,96},{192,128},{224,160},{256,192},{28... | collective-permute-start | bytes 6152 | tf_op jit(solution)/shard_map/ppermute | solution.py:27
  11.2 0.0 collective-permute-done.list1_ref
  11.2 4.4 %collective-permute-done.1.list2_ref = s32[1,512]{1,0:T(1,128)S(1)} collective-permute-done((s32[1,512]{1,0:T(1,128)S(1)}, s32[1,512]{1,0:T(1,128)S(1)}, u32[]{:S(2)}, u32[]{:S(2)}) %collective-permute-start.1) | collective-permute-done | bytes 2080 | tf_op jit(solution)/shard_map/ppermute | solution.py:27
  15.6 1.2 %copy-done = f32[16,16,1024]{2,1,0:T(8,128)S(1)} copy-done((f32[16,16,1024]{2,1,0:T(8,128)S(1)}, f32[16,16,1024]{2,1,0:T(8,128)}, u32[]{:S(2)}) %copy-start) | copy-done | bytes 1048600
  16.9 1.5 %serve.1 = (f32[512,128]{1,0:T(8,128)S(1)}, f32[512,128]{1,0:T(8,128)S(1)}) custom-call(s32[1,512]{1,0:T(1,128)S(1)} %collective-permute-done.list1_ref, s32[1,512]{1,0:T(1,128)S(1)} %collective-permute-done.1.list2_ref, f32[2048,128]{1,0:T(8,128)S(1)} %bitcast.24), custom_call_target="tpu_custom_call" | custom-call | tf_op jit(solution)/shard_map/serve/pallas_call | solution.py:116
  18.4 0.0 copy-start.2
  18.4 2.1 %collective-permute-start.2 = (f32[512,128]{1,0:T(8,128)S(1)}, f32[512,128]{1,0:T(8,128)S(1)}, u32[]{:S(2)}, u32[]{:S(2)}) collective-permute-start(f32[512,128]{1,0:T(8,128)S(1)} %get-tuple-element.27), channel_id=1, source_target_pairs={{0,32},{32,64},{64,96},{96,128},{128,160},{160,192},{192,224},{224... | collective-permute-start | bytes 786440 | tf_op jit(solution)/shard_map/ppermute | solution.py:27
  20.5 1.9 %collective-permute-start.3 = (f32[512,128]{1,0:T(8,128)S(1)}, f32[512,128]{1,0:T(8,128)S(1)}, u32[]{:S(2)}, u32[]{:S(2)}) collective-permute-start(f32[512,128]{1,0:T(8,128)S(1)} %get-tuple-element.28), channel_id=1, source_target_pairs={{0,64},{32,96},{64,128},{96,160},{128,192},{160,224},{192,256},{22... | collective-permute-start | bytes 786440 | tf_op jit(solution)/shard_map/ppermute | solution.py:27
  22.4 0.0 copy-start.4
  22.4 1.0 %copy-done.4 = f32[8,128,128]{2,1,0:T(8,128)S(1)} copy-done((f32[8,128,128]{2,1,0:T(8,128)S(1)}, f32[8,128,128]{2,1,0:T(8,128)}, u32[]{:S(2)}) %copy-start.4) | copy-done | bytes 524312
  23.5 1.5 %coefficients.1 = (f32[80,128]{1,0:T(8,128)S(1)}, f32[6,32,128]{2,1,0:T(8,128)S(1)}, bf16[32,384]{1,0:T(8,128)(2,1)S(1)}) custom-call(f32[4,128]{1,0:T(4,128)S(1)} %bitcast.31, f32[8,128,128]{2,1,0:T(8,128)S(1)} %copy-done.4), custom_call_target="tpu_custom_call" | custom-call | flops 8000000 | bytes 4000000 | tf_op jit(solution)/shard_map/coefficients/pallas_call | solution.py:192
  25.0 4.4 %before_arrival.1 = (f32[2056,128]{1,0:T(8,128)S(1)}, f32[2048,384]{1,0:T(8,128)S(1)}, s32[1,512]{1,0:T(1,128)S(1)}, s32[1,512]{1,0:T(1,128)S(1)}) custom-call(s32[16,128]{1,0:T(8,128)S(1)} %get-tuple-element.20.place_ref, f32[2048,128]{1,0:T(8,128)S(1)} %bitcast.25, s32[16,128]{1,0:T(8,128)S(1)} %get-tuple-element.21.shift_ref, s32[16,8,16]{2,1,0:T(8,128)S(1)} %bitcast.28, ...), custom_call_target="tpu_custom_call" | custom-call | flops 20000000 | bytes 10000000 | tf_op jit(solution)/shard_map/before_arrival/pallas_call | solution.py:243
  29.5 3.9 %collective-permute-done.2.got1_ref = f32[512,128]{1,0:T(8,128)S(1)} collective-permute-done((f32[512,128]{1,0:T(8,128)S(1)}, f32[512,128]{1,0:T(8,128)S(1)}, u32[]{:S(2)}, u32[]{:S(2)}) %collective-permute-start.2) | collective-permute-done | bytes 262176 | tf_op jit(solution)/shard_map/ppermute | solution.py:27
  33.4 1.4 %collective-permute-done.3.got2_ref = f32[512,128]{1,0:T(8,128)S(1)} collective-permute-done((f32[512,128]{1,0:T(8,128)S(1)}, f32[512,128]{1,0:T(8,128)S(1)}, u32[]{:S(2)}, u32[]{:S(2)}) %collective-permute-start.3) | collective-permute-done | bytes 262176 | tf_op jit(solution)/shard_map/ppermute | solution.py:27
  34.8 1.2 %copy-done.3 = f32[16,16,1024]{2,1,0:T(8,128)S(1)} copy-done((f32[16,16,1024]{2,1,0:T(8,128)S(1)}, f32[16,16,1024]{2,1,0:T(8,128)}, u32[]{:S(2)}) %copy-start.3) | copy-done | bytes 1048600
  36.0 3.9 %slab.1 = (f32[2048,128]{1,0:T(8,128)S(1)}, f32[32,8,128]{2,1,0:T(8,128)S(1)}, f32[2056,128]{1,0:T(8,128)S(1)}) custom-call(s32[1,512]{1,0:T(1,128)S(1)} %get-tuple-element.23.to1_ref, s32[1,512]{1,0:T(1,128)S(1)} %get-tuple-element.24.to2_ref, f32[512,128]{1,0:T(8,128)S(1)} %collective-permute-done.2.got1_ref, ...), custom_call_target="tpu_custom_call", output_to_operand_aliasing={{2}: (4, {})} | custom-call | tf_op jit(solution)/shard_map/slab/pallas_call | solution.py:311
  39.9 32.5 %all_to_all.10.ends_ref = f32[32,8,128]{2,1,0:T(8,128)S(1)} all-to-all(f32[32,8,128]{2,1,0:T(8,128)S(1)} %get-tuple-element.33), channel_id=1, replica_groups=mesh['gx'=16,'gy'=32] {'gy'}, dimensions={0} | all-to-all | bytes 262144 | tf_op jit(solution)/shard_map/all_to_all | solution.py:399
  72.4 0.2 interface.1
  72.5 20.2 %all_to_all.11.near_ref = f32[32,8,128]{2,1,0:T(8,128)S(1)} all-to-all(f32[32,8,128]{2,1,0:T(8,128)S(1)} %interface.1), channel_id=1, replica_groups=mesh['gx'=16,'gy'=32] {'gy'}, dimensions={0} | all-to-all | bytes 262144 | tf_op jit(solution)/shard_map/all_to_all | solution.py:401
  92.7 1.2 %finish.1 = f32[2048,128]{1,0:T(8,128)} custom-call(f32[2048,128]{1,0:T(8,128)S(1)} %get-tuple-element.32.base_ref, f32[32,8,128]{2,1,0:T(8,128)S(1)} %all_to_all.11.near_ref, f32[80,128]{1,0:T(8,128)S(1)} %get-tuple-element.31.own_ref), custom_call_target="tpu_custom_call" | custom-call | tf_op jit(solution)/shard_map/finish/pallas_call | solution.py:373
  (11 shorter events, 0.0 us)
Async XLA Ops:
  0.0 25.0 %copy-start.5 = (s32[16,16,8]{1,2,0:T(8,128)S(1)}, s32[16,16,8]{1,2,0:T(8,128)}, u32[]{:S(2)}) copy-start(s32[16,16,8]{1,2,0:T(8,128)} %param.14) | copy-start | bytes 24580
  0.0 0.9 copy-start.6
  0.9 0.8 copy-start.7
  1.7 20.7 %copy-start.8 = (f32[512]{0:T(512)S(1)}, f32[512]{0:T(512)}, u32[]{:S(2)}) copy-start(f32[512]{0:T(512)} %param.11) | copy-start | bytes 6148
  3.5 7.7 %collective-permute-start = (s32[1,512]{1,0:T(1,128)S(1)}, s32[1,512]{1,0:T(1,128)S(1)}, u32[]{:S(2)}, u32[]{:S(2)}) collective-permute-start(s32[1,512]{1,0:T(1,128)S(1)} %get-tuple-element.25), channel_id=1, source_target_pairs={{32,0},{64,32},{96,64},{128,96},{160,128},{192,160},{224,192},{256... | collective-permute-start | bytes 6152 | tf_op jit(solution)/shard_map/ppermute | solution.py:27
  8.7 7.0 %collective-permute-start.1 = (s32[1,512]{1,0:T(1,128)S(1)}, s32[1,512]{1,0:T(1,128)S(1)}, u32[]{:S(2)}, u32[]{:S(2)}) collective-permute-start(s32[1,512]{1,0:T(1,128)S(1)} %get-tuple-element.26), channel_id=1, source_target_pairs={{64,0},{96,32},{128,64},{160,96},{192,128},{224,160},{256,192},{28... | collective-permute-start | bytes 6152 | tf_op jit(solution)/shard_map/ppermute | solution.py:27
  15.6 1.2 %copy-start = (f32[16,16,1024]{2,1,0:T(8,128)S(1)}, f32[16,16,1024]{2,1,0:T(8,128)}, u32[]{:S(2)}) copy-start(f32[16,16,1024]{2,1,0:T(8,128)} %param.8) | copy-start | bytes 3145732
  16.9 8.2 %copy-start.1 = (f32[16,16,1024]{2,1,0:T(8,128)S(1)}, f32[16,16,1024]{2,1,0:T(8,128)}, u32[]{:S(2)}) copy-start(f32[16,16,1024]{2,1,0:T(8,128)} %param.8) | copy-start | bytes 3145732
  18.4 16.4 %copy-start.2 = (f32[16,16,1024]{2,1,0:T(8,128)S(1)}, f32[16,16,1024]{2,1,0:T(8,128)}, u32[]{:S(2)}) copy-start(f32[16,16,1024]{2,1,0:T(8,128)} %param.9) | copy-start | bytes 3145732
  18.4 14.9 %collective-permute-start.2 = (f32[512,128]{1,0:T(8,128)S(1)}, f32[512,128]{1,0:T(8,128)S(1)}, u32[]{:S(2)}, u32[]{:S(2)}) collective-permute-start(f32[512,128]{1,0:T(8,128)S(1)} %get-tuple-element.27), channel_id=1, source_target_pairs={{0,32},{32,64},{64,96},{96,128},{128,160},{160,192},{192,224},{224... | collective-permute-start | bytes 786440 | tf_op jit(solution)/shard_map/ppermute | solution.py:27
  20.5 14.3 %collective-permute-start.3 = (f32[512,128]{1,0:T(8,128)S(1)}, f32[512,128]{1,0:T(8,128)S(1)}, u32[]{:S(2)}, u32[]{:S(2)}) collective-permute-start(f32[512,128]{1,0:T(8,128)S(1)} %get-tuple-element.28), channel_id=1, source_target_pairs={{0,64},{32,96},{64,128},{96,160},{128,192},{160,224},{192,256},{22... | collective-permute-start | bytes 786440 | tf_op jit(solution)/shard_map/ppermute | solution.py:27
  22.4 1.0 %copy-start.4 = (f32[8,128,128]{2,1,0:T(8,128)S(1)}, f32[8,128,128]{2,1,0:T(8,128)}, u32[]{:S(2)}) copy-start(f32[8,128,128]{2,1,0:T(8,128)} %mats_ref.1) | copy-start | bytes 1572868
  34.8 1.2 %copy-start.3 = (f32[16,16,1024]{2,1,0:T(8,128)S(1)}, f32[16,16,1024]{2,1,0:T(8,128)}, u32[]{:S(2)}) copy-start(f32[16,16,1024]{2,1,0:T(8,128)} %param.10) | copy-start | bytes 3145732

commit v3 on v2

--- a/solution.py
+++ b/solution.py
@@ -14,6 +14,7 @@
 HIGH = lax.Precision.HIGHEST
 VMEM = pl.BlockSpec(memory_space=pltpu.VMEM)
 SMEM = pl.BlockSpec(memory_space=pltpu.SMEM)
+ANY = pl.BlockSpec(memory_space=pl.ANY)
 PARAMS = pltpu.CompilerParams(vmem_limit_bytes=24 << 20)
 
 
@@ -25,6 +26,10 @@
     peers = lax.axis_size(axis)
     pairs = [(i, i + by) for i in range(peers) if 0 <= i + by < peers]
     return lax.ppermute(value, axis, pairs)
+
+
+def far(value):
+    return pltpu.with_memory_space_constraint(value, pltpu.HBM)
 
 
 def to_rows(value):
@@ -72,7 +77,11 @@
     return (total[0:1, :] + empty).astype(jnp.int32)
 
 
-def request_kernel(shift_ref, tile_ref, list1_ref, list2_ref, place_ref, shift_out, picked_ref):
+def request_kernel(
+    shift_ref, tile_ref, rows_hbm, list1_ref, list2_ref, place_ref, shift_out, rows_ref, picked_ref, sem
+):
+    copy = pltpu.make_async_copy(rows_hbm, rows_ref, sem)
+    copy.start()
     shift, tile = by_lanes(shift_ref), by_lanes(tile_ref)
     place = (tile & -64) | ((tile & 7) << 3) | (lax.shift_right_logical(tile, 3) & 7)
     place_ref[...] = place
@@ -80,9 +89,10 @@
     place = place.astype(jnp.float32)
     for step, list_ref in ((1, list1_ref), (2, list2_ref)):
         list_ref[...] = compact(ranks_of(shift == step), place, 0.0, picked_ref)
-
-
-def request(shift, tile):
+    copy.wait()
+
+
+def request(shift, tile, rows):
     return pl.pallas_call(
         request_kernel,
         out_shape=(
@@ -90,37 +100,35 @@
             pltpu.VMEM((1, CAP), jnp.int32),
             jax.ShapeDtypeStruct((PLANES, LANES), jnp.int32),
             pltpu.VMEM((PLANES, LANES), jnp.int32),
+            pltpu.VMEM((TILES, LANES), jnp.float32),
         ),
-        in_specs=[VMEM] * 2,
-        out_specs=[VMEM] * 4,
-        scratch_shapes=[pltpu.VMEM((CAP, LANES), jnp.float32)],
+        in_specs=[VMEM] * 2 + [ANY],
+        out_specs=[VMEM] * 5,
+        scratch_shapes=[pltpu.VMEM((CAP, LANES), jnp.float32), pltpu.SemaphoreType.DMA],
         compiler_params=PARAMS,
         name="request",
-    )(near(shift), near(tile))
-
-
-def serve_kernel(list1_ref, list2_ref, rows_ref, out1_ref, out2_ref):
-    for list_ref, out_ref in ((list1_ref, out1_ref), (list2_ref, out2_ref)):
-
-        def step(k, carry, list_ref=list_ref, out_ref=out_ref):
-            for j in range(32):
-                slot = k * 32 + j
-                out_ref[pl.ds(slot, 1), :] = rows_ref[pl.ds(list_ref[0, slot], 1), :]
-            return carry
-
-        lax.fori_loop(0, CAP // 32, step, 0)
-
-
-def serve(list1, list2, rows):
-    out = pltpu.VMEM((CAP, LANES), jnp.float32)
+    )(far(shift), far(tile), far(rows))
+
+
+def serve_kernel(list_ref, rows_ref, out_ref):
+    def step(k, carry):
+        for j in range(32):
+            slot = k * 32 + j
+            out_ref[pl.ds(slot, 1), :] = rows_ref[pl.ds(list_ref[0, slot], 1), :]
+        return carry
+
+    lax.fori_loop(0, CAP // 32, step, 0)
+
+
+def serve(wanted, rows):
     return pl.pallas_call(
         serve_kernel,
-        out_shape=(out, out),
-        in_specs=[SMEM] * 2 + [VMEM],
-        out_specs=[VMEM] * 2,
+        out_shape=pltpu.VMEM((CAP, LANES), jnp.float32),
+        in_specs=[SMEM, VMEM],
+        out_specs=VMEM,
         compiler_params=PARAMS,
         name="serve",
-    )(list1, list2, rows)
+    )(wanted, near(rows))
 
 
 def coef_kernel(diff_ref, mats_ref, own_ref, red_ref, diag_ref, own_t, row_t):
@@ -205,12 +213,19 @@
         compiler_params=PARAMS,
         cost_estimate=pl.CostEstimate(flops=8_000_000, bytes_accessed=4_000_000, transcendentals=0),
         name="coefficients",
-    )(diffusivity.reshape(-1, LANES), near(mats))
+    )(diffusivity.reshape(-1, LANES), mats)
 
 
 def local_kernel(
-    place_ref, rows_ref, shift_ref, class_ref, diag_ref, dep_ref, weights_ref, to1_ref, to2_ref, picked_ref
+    place_ref, rows_ref, shift_ref, class_ref, diag_ref, one_hbm, two_hbm,
+    dep_ref, weights_ref, to1_ref, to2_ref, one_ref, two_ref, picked_ref, sems,
 ):
+    copies = [
+        pltpu.make_async_copy(one_hbm, one_ref, sems.at[0]),
+        pltpu.make_async_copy(two_hbm, two_ref, sems.at[1]),
+    ]
+    for copy in copies:
+        copy.start()
     shift = shift_ref[...]
     spot = iota((PLANES, LANES), 1)
     spot = ((spot & 8) << 3) | (lax.shift_right_logical(spot, 4) << 3) | (spot & 7)
@@ -237,9 +252,11 @@
         return carry
 
     lax.fori_loop(0, PLANES, plane, 0)
-
-
-def before_arrival(place, rows, shift, classes, diag):
+    for copy in copies:
+        copy.wait()
+
+
+def before_arrival(place, rows, shift, classes, diag, one, two):
     return pl.pallas_call(
         local_kernel,
         out_shape=(
@@ -247,30 +264,46 @@
             pltpu.VMEM((TILES, 3 * LANES), jnp.float32),
             jax.ShapeDtypeStruct((1, CAP), jnp.int32),
             jax.ShapeDtypeStruct((1, CAP), jnp.int32),
+            pltpu.VMEM((TILES, LANES), jnp.float32),
+            pltpu.VMEM((TILES, LANES), jnp.float32),
         ),
-        in_specs=[SMEM] + [VMEM] * 4,
-        out_specs=[VMEM] * 4,
-        scratch_shapes=[pltpu.VMEM((CAP, LANES), jnp.float32)],
+        in_specs=[SMEM] + [VMEM] * 4 + [ANY] * 2,
+        out_specs=[VMEM] * 6,
+        scratch_shapes=[pltpu.VMEM((CAP, LANES), jnp.float32), pltpu.SemaphoreType.DMA((2,))],
         compiler_params=PARAMS,
         cost_estimate=pl.CostEstimate(flops=20_000_000, bytes_accessed=10_000_000, transcendentals=0),
         name="before_arrival",
-    )(place, rows, near(shift), near(classes), near(diag))
+    )(place, near(rows), near(shift), classes, near(diag), far(one), far(two))
+
+
+def patch_kernel(to_ref, got_ref, dep_in, dep_ref):
+    del dep_in
+
+    def patch(k, carry):
+        start = pl.multiple_of(k * 32, 32)
+        for j in range(32):
+            dep_ref[pl.ds(to_ref[0, start + j], 1), :] = got_ref[pl.ds(start + j, 1), :]
+        return carry
+
+    lax.fori_loop(0, CAP // 32, patch, 0)
+
+
+def patched(to, got, dep):
+    return pl.pallas_call(
+        patch_kernel,
+        out_shape=pltpu.VMEM(dep.shape, jnp.float32),
+        in_specs=[SMEM] + [VMEM] * 2,
+        out_specs=VMEM,
+        input_output_aliases={2: 0},
+        compiler_params=PARAMS,
+        name="patch",
+    )(to, near(got), near(dep))
 
 
 def slab_kernel(
-    to1_ref, to2_ref, got1_ref, got2_ref, dep_in, weights_ref, one_ref, two_ref, own_ref,
-    base_ref, ends_ref, dep_ref, partial,
+    to_ref, got_ref, dep_in, weights_ref, one_ref, two_ref, own_ref, base_ref, ends_ref, dep_ref, partial
 ):
-    del dep_in
-    for to_ref, got_ref in ((to1_ref, got1_ref), (to2_ref, got2_ref)):
-
-        def patch(k, carry, to_ref=to_ref, got_ref=got_ref):
-            start = pl.multiple_of(k * 32, 32)
-            for j in range(32):
-                dep_ref[pl.ds(to_ref[0, start + j], 1), :] = got_ref[pl.ds(start + j, 1), :]
-            return carry
-
-        lax.fori_loop(0, CAP // 32, patch, 0)
+    patch_kernel(to_ref, got_ref, dep_in, dep_ref)
 
     def own(kind, z):
         return own_ref[pl.ds(kind * PLANES + z, 1), :]
@@ -307,7 +340,7 @@
         ends_ref[d, pl.ds(share, share), :] = last[d * share : (d + 1) * share, :]
 
 
-def slab(to1, to2, got1, got2, dep, weights, one, two, own, devices):
+def slab(to, got, dep, weights, one, two, own, devices):
     base, ends, _ = pl.pallas_call(
         slab_kernel,
         out_shape=(
@@ -315,13 +348,13 @@
             pltpu.VMEM((devices, 2 * ROWS // devices, LANES), jnp.float32),
             pltpu.VMEM((TILES + 8, LANES), jnp.float32),
         ),
-        in_specs=[SMEM] * 2 + [VMEM] * 7,
+        in_specs=[SMEM] + [VMEM] * 6,
         out_specs=[VMEM] * 3,
         scratch_shapes=[pltpu.VMEM((TILES, LANES), jnp.float32)],
-        input_output_aliases={4: 2},
+        input_output_aliases={2: 2},
         compiler_params=PARAMS,
         name="slab",
-    )(to1, to2, near(got1), near(got2), near(dep), near(weights), near(one), near(two), near(own))
+    )(to, near(got), near(dep), near(weights), near(one), near(two), near(own))
     return base, ends
 
 
@@ -385,17 +418,17 @@
     conc, target_one, target_two, diffusivity, src_shift, src_tile, interp_class, interp_mats
 ):
     devices = lax.axis_size("gy")
-    rows = near(to_rows(conc))
     as_stored = lambda value: value.transpose(0, 2, 1)
-    list1, list2, place, shift = request(as_stored(src_shift), as_stored(src_tile))
-    asked1, asked2 = shifted(list1, "gx", -1), shifted(list2, "gx", -2)
+    list1, list2, place, shift, rows = request(as_stored(src_shift), as_stored(src_tile), to_rows(conc))
+    asked2, asked1 = shifted(list2, "gx", -2), shifted(list1, "gx", -1)
     own, red, diag = coefficients(diffusivity, interp_mats, devices)
-    send1, send2 = serve(asked1, asked2, rows)
-    got1, got2 = shifted(send1, "gx", 1), shifted(send2, "gx", 2)
-    dep, weights, to1, to2 = before_arrival(place, rows, shift, as_stored(interp_class), diag)
-    base, ends = slab(
-        to1, to2, got1, got2, dep, weights, to_rows(target_one), to_rows(target_two), own, devices
+    got2 = shifted(serve(asked2, rows), "gx", 2)
+    got1 = shifted(serve(asked1, rows), "gx", 1)
+    dep, weights, to1, to2, one, two = before_arrival(
+        place, rows, shift, as_stored(interp_class), diag, to_rows(target_one), to_rows(target_two)
     )
+    dep = patched(to1, got1, dep)
+    base, ends = slab(to2, got2, dep, weights, one, two, own, devices)
     ends = lax.all_to_all(ends, "gy", split_axis=0, concat_axis=0, tiled=True)
     sides = interface(ends, red)
     sides = lax.all_to_all(sides, "gy", split_axis=0, concat_axis=0, tiled=True)

time: 94.3 us -> 86.3 us (0.915)
  waiting for transfers between devices: 9.74 us -> 2.53 us
  local copies, waits for them, and re-layouts: 5.21 us -> 0.02 us
  starting transfers between devices: 11.7 us -> 14.3 us
  Pallas kernels: 14.4 us -> 16.4 us
    ppermute x4, waiting for transfers between devices: 9.74 us -> 2.53 us  [shifted(): return lax.ppermute(value, axis, pairs)]
    unnamed x18 -> x6, local copies, waits for them, and re-layouts: 5.21 us -> 0.02 us
    ppermute x4, starting transfers between devices: 11.7 us -> 14.3 us  [shifted(): return lax.ppermute(value, axis, pairs)]
    pallas_call x1 -> x3, Pallas kernels: 1.54 us -> 3.12 us  [the longest x2 2.08 us: serve(): pl.pallas_call(serve_kernel, out_shape=pltpu.VMEM((CAP, LANES), jnp.float...]
  transfers between devices with their start and end apart: 4 -> 4, of which waited for: 3 -> 2; matrix products, arithmetic and copies ran while one was open for 0% -> 0% of each run, Pallas kernels for 6% -> 11%
where the time goes in v3:
time: 86.3 us; the launch traced here: 86 us
  blocking collectives  52.6 us (61%)
  Pallas kernels  16.4 us (19%)
  starting transfers between devices  14.3 us (17%)
  waiting for transfers between devices  2.53 us (3%)
    all_to_all x1, blocking collectives, local(): ends = lax.all_to_all(ends, 'gy', split_axis=0, concat_axis=0, tiled=True)  32.5 us
    all_to_all x1, blocking collectives, local(): sides = lax.all_to_all(sides, 'gy', split_axis=0, concat_axis=0, tiled=True)  20.2 us
    ppermute x4, starting transfers between devices, shifted(): return lax.ppermute(value, axis, pairs)  14.3 us
    pallas_call x1, Pallas kernels, before_arrival(): pl.pallas_call(local_kernel, out_shape=(pltpu.VMEM((TILES + 8, LANES), jn...  4.47 us
    pallas_call x1, Pallas kernels, slab(): pl.pallas_call(slab_kernel, out_shape=(pltpu.VMEM((TILES, LANES), jnp.flo...  3.31 us
    pallas_call x1, Pallas kernels, request(): pl.pallas_call(request_kernel, out_shape=(pltpu.VMEM((1, CAP), jnp.int32)...  2.64 us
    ppermute x4, waiting for transfers between devices, shifted(): return lax.ppermute(value, axis, pairs)  2.53 us
    pallas_call x2, Pallas kernels, serve(): pl.pallas_call(serve_kernel, out_shape=pltpu.VMEM((CAP, LANES), jnp.float...  2.08 us
  transfers between devices with their start and end apart: 4, of which 2 were waited for; matrix products, arithmetic and copies ran while one was open for 0% of the time, Pallas kernels for 11%

profile of v3, /device:TPU:6, one launch (start us, length us, event | category | flops | bytes accessed | tf_op | source)
XLA Modules:
  0.0 86.0 jit_solution(949154251404366292)
XLA Ops:
  0.0 2.6 %request.1 = (s32[1,512]{1,0:T(1,128)S(1)}, s32[1,512]{1,0:T(1,128)S(1)}, s32[16,128]{1,0:T(8,128)S(1)}, s32[16,128]{1,0:T(8,128)S(1)}, f32[2048,128]{1,0:T(8,128)S(1)}) custom-call(s32[16,8,16]{2,1,0:T(8,128)} %bitcast.29, s32[16,8,16]{2,1,0:T(8,128)} %bitcast.30, f32[2048,128]{1,0:T(8,128)} %bitcast.28), custom_call_target="tpu_custom_call" | custom-call | tf_op jit(solution)/shard_map/request/pallas_call | solution.py:96
  2.6 5.2 %collective-permute-start.2 = (s32[1,512]{1,0:T(1,128)S(1)}, s32[1,512]{1,0:T(1,128)S(1)}, u32[]{:S(2)}, u32[]{:S(2)}) collective-permute-start(s32[1,512]{1,0:T(1,128)S(1)} %get-tuple-element.28), channel_id=1, source_target_pairs={{32,0},{64,32},{96,64},{128,96},{160,128},{192,160},{224,192},{256... | collective-permute-start | bytes 6152 | tf_op jit(solution)/shard_map/ppermute | solution.py:28
  7.8 2.5 %collective-permute-start = (s32[1,512]{1,0:T(1,128)S(1)}, s32[1,512]{1,0:T(1,128)S(1)}, u32[]{:S(2)}, u32[]{:S(2)}) collective-permute-start(s32[1,512]{1,0:T(1,128)S(1)} %get-tuple-element.26), channel_id=1, source_target_pairs={{64,0},{96,32},{128,64},{160,96},{192,128},{224,160},{256,192},{28... | collective-permute-start | bytes 6152 | tf_op jit(solution)/shard_map/ppermute | solution.py:28
  10.4 0.0 collective-permute-done.2.list_ref
  10.4 0.0 copy-start
  10.4 0.0 copy-start.2
  10.4 1.0 %serve.3 = f32[512,128]{1,0:T(8,128)S(1)} custom-call(s32[1,512]{1,0:T(1,128)S(1)} %collective-permute-done.2.list_ref, f32[2048,128]{1,0:T(8,128)S(1)} %get-tuple-element.22.rows_ref), custom_call_target="tpu_custom_call" | custom-call | tf_op jit(solution)/shard_map/serve/pallas_call | solution.py:124
  11.5 0.0 copy-start.1
  11.5 3.0 %collective-permute-start.3 = (f32[512,128]{1,0:T(8,128)S(1)}, f32[512,128]{1,0:T(8,128)S(1)}, u32[]{:S(2)}, u32[]{:S(2)}) collective-permute-start(f32[512,128]{1,0:T(8,128)S(1)} %serve.3), channel_id=1, source_target_pairs={{0,32},{32,64},{64,96},{96,128},{128,160},{160,192},{192,224},{224... | collective-permute-start | bytes 786440 | tf_op jit(solution)/shard_map/ppermute | solution.py:28
  14.5 0.3 collective-permute-done.list_ref
  14.8 1.0 %serve.2 = f32[512,128]{1,0:T(8,128)S(1)} custom-call(s32[1,512]{1,0:T(1,128)S(1)} %collective-permute-done.list_ref, f32[2048,128]{1,0:T(8,128)S(1)} %get-tuple-element.22.rows_ref), custom_call_target="tpu_custom_call" | custom-call | tf_op jit(solution)/shard_map/serve/pallas_call | solution.py:124
  15.9 3.5 %collective-permute-start.1 = (f32[512,128]{1,0:T(8,128)S(1)}, f32[512,128]{1,0:T(8,128)S(1)}, u32[]{:S(2)}, u32[]{:S(2)}) collective-permute-start(f32[512,128]{1,0:T(8,128)S(1)} %serve.2), channel_id=1, source_target_pairs={{0,64},{32,96},{64,128},{96,160},{128,192},{160,224},{192,256},{22... | collective-permute-start | bytes 786440 | tf_op jit(solution)/shard_map/ppermute | solution.py:28
  19.4 0.0 copy-done
  19.4 0.0 copy-done.2
  19.4 1.5 %coefficients.1 = (f32[80,128]{1,0:T(8,128)S(1)}, f32[6,32,128]{2,1,0:T(8,128)S(1)}, bf16[32,384]{1,0:T(8,128)(2,1)S(1)}) custom-call(f32[4,128]{1,0:T(4,128)S(1)} %bitcast.25, f32[8,128,128]{2,1,0:T(8,128)S(1)} %copy-done), custom_call_target="tpu_custom_call" | custom-call | flops 8000000 | bytes 4000000 | tf_op jit(solution)/shard_map/coefficients/pallas_call | solution.py:200
  21.0 4.5 %before_arrival.1 = (f32[2056,128]{1,0:T(8,128)S(1)}, f32[2048,384]{1,0:T(8,128)S(1)}, s32[1,512]{1,0:T(1,128)S(1)}, s32[1,512]{1,0:T(1,128)S(1)}, f32[2048,128]{1,0:T(8,128)S(1)}, /*index=5*/f32[2048,128]{1,0:T(8,128)S(1)}) custom-call(s32[16,128]{1,0:T(8,128)S(1)} %get-tuple-element.21.place_ref, f32[2048,128]{1,0:T(8,128)S(1)} %get-tuple-element.22.rows_ref, ...), custom_call_target="tpu_custom_call" | custom-call | flops 20000000 | bytes 10000000 | tf_op jit(solution)/shard_map/before_arrival/pallas_call | solution.py:260
  25.5 0.0 collective-permute-done.3.got_ref
  25.5 1.0 %patch.1.dep_in = f32[2056,128]{1,0:T(8,128)S(1)} custom-call(s32[1,512]{1,0:T(1,128)S(1)} %get-tuple-element.27.to_ref, f32[512,128]{1,0:T(8,128)S(1)} %collective-permute-done.3.got_ref, f32[2056,128]{1,0:T(8,128)S(1)} %get-tuple-element.29.dep_in), custom_call_target="tpu_custom_call", output_to_operand_aliasing={{}: (2, {})} | custom-call | tf_op jit(solution)/shard_map/patch/pallas_call | solution.py:292
  26.5 2.2 %collective-permute-done.1.got_ref = f32[512,128]{1,0:T(8,128)S(1)} collective-permute-done((f32[512,128]{1,0:T(8,128)S(1)}, f32[512,128]{1,0:T(8,128)S(1)}, u32[]{:S(2)}, u32[]{:S(2)}) %collective-permute-start.1) | collective-permute-done | bytes 262176 | tf_op jit(solution)/shard_map/ppermute | solution.py:28
  28.7 3.3 %slab.1 = (f32[2048,128]{1,0:T(8,128)S(1)}, f32[32,8,128]{2,1,0:T(8,128)S(1)}, f32[2056,128]{1,0:T(8,128)S(1)}) custom-call(s32[1,512]{1,0:T(1,128)S(1)} %get-tuple-element.25.to_ref, f32[512,128]{1,0:T(8,128)S(1)} %collective-permute-done.1.got_ref, f32[2056,128]{1,0:T(8,128)S(1)} %patch.1.dep_in, ...), custom_call_target="tpu_custom_call", output_to_operand_aliasing={{2}: (2, {})} | custom-call | tf_op jit(solution)/shard_map/slab/pallas_call | solution.py:344
  32.0 32.5 %all_to_all.10.ends_ref = f32[32,8,128]{2,1,0:T(8,128)S(1)} all-to-all(f32[32,8,128]{2,1,0:T(8,128)S(1)} %get-tuple-element.35), channel_id=1, replica_groups=mesh['gx'=16,'gy'=32] {'gy'}, dimensions={0} | all-to-all | bytes 262144 | tf_op jit(solution)/shard_map/all_to_all | solution.py:432
  64.5 0.2 interface.1
  64.7 20.2 %all_to_all.11.near_ref = f32[32,8,128]{2,1,0:T(8,128)S(1)} all-to-all(f32[32,8,128]{2,1,0:T(8,128)S(1)} %interface.1), channel_id=1, replica_groups=mesh['gx'=16,'gy'=32] {'gy'}, dimensions={0} | all-to-all | bytes 262144 | tf_op jit(solution)/shard_map/all_to_all | solution.py:434
  84.8 1.2 %finish.1 = f32[2048,128]{1,0:T(8,128)} custom-call(f32[2048,128]{1,0:T(8,128)S(1)} %get-tuple-element.34.base_ref, f32[32,8,128]{2,1,0:T(8,128)S(1)} %all_to_all.11.near_ref, f32[80,128]{1,0:T(8,128)S(1)} %get-tuple-element.33.own_ref), custom_call_target="tpu_custom_call" | custom-call | tf_op jit(solution)/shard_map/finish/pallas_call | solution.py:406
  (1 shorter events, 0.0 us)
Async XLA Ops:
  2.6 7.7 %collective-permute-start.2 = (s32[1,512]{1,0:T(1,128)S(1)}, s32[1,512]{1,0:T(1,128)S(1)}, u32[]{:S(2)}, u32[]{:S(2)}) collective-permute-start(s32[1,512]{1,0:T(1,128)S(1)} %get-tuple-element.28), channel_id=1, source_target_pairs={{32,0},{64,32},{96,64},{128,96},{160,128},{192,160},{224,192},{256... | collective-permute-start | bytes 6152 | tf_op jit(solution)/shard_map/ppermute | solution.py:28
  7.8 7.0 %collective-permute-start = (s32[1,512]{1,0:T(1,128)S(1)}, s32[1,512]{1,0:T(1,128)S(1)}, u32[]{:S(2)}, u32[]{:S(2)}) collective-permute-start(s32[1,512]{1,0:T(1,128)S(1)} %get-tuple-element.26), channel_id=1, source_target_pairs={{64,0},{96,32},{128,64},{160,96},{192,128},{224,160},{256,192},{28... | collective-permute-start | bytes 6152 | tf_op jit(solution)/shard_map/ppermute | solution.py:28
  10.4 9.0 %copy-start = (f32[8,128,128]{2,1,0:T(8,128)S(1)}, f32[8,128,128]{2,1,0:T(8,128)}, u32[]{:S(2)}) copy-start(f32[8,128,128]{2,1,0:T(8,128)} %mats_ref.1) | copy-start | bytes 1572868
  10.4 9.0 %copy-start.2 = (f32[512]{0:T(512)S(1)}, f32[512]{0:T(512)}, u32[]{:S(2)}) copy-start(f32[512]{0:T(512)} %param.11) | copy-start | bytes 6148
  11.5 9.5 %copy-start.1 = (s32[16,16,8]{1,2,0:T(8,128)S(1)}, s32[16,16,8]{1,2,0:T(8,128)}, u32[]{:S(2)}) copy-start(s32[16,16,8]{1,2,0:T(8,128)} %param.14) | copy-start | bytes 24580
  11.5 14.0 %collective-permute-start.3 = (f32[512,128]{1,0:T(8,128)S(1)}, f32[512,128]{1,0:T(8,128)S(1)}, u32[]{:S(2)}, u32[]{:S(2)}) collective-permute-start(f32[512,128]{1,0:T(8,128)S(1)} %serve.3), channel_id=1, source_target_pairs={{0,32},{32,64},{64,96},{96,128},{128,160},{160,192},{192,224},{224... | collective-permute-start | bytes 786440 | tf_op jit(solution)/shard_map/ppermute | solution.py:28
  15.9 12.8 %collective-permute-start.1 = (f32[512,128]{1,0:T(8,128)S(1)}, f32[512,128]{1,0:T(8,128)S(1)}, u32[]{:S(2)}, u32[]{:S(2)}) collective-permute-start(f32[512,128]{1,0:T(8,128)S(1)} %serve.2), channel_id=1, source_target_pairs={{0,64},{32,96},{64,128},{96,160},{128,192},{160,224},{192,256},{22... | collective-permute-start | bytes 786440 | tf_op jit(solution)/shard_map/ppermute | solution.py:28

commit v4 on v3

--- a/solution.py
+++ b/solution.py
@@ -11,6 +11,7 @@
 ROWS = 128
 TILES = PLANES * ROWS
 CAP = 512
+GROUP = 8
 HIGH = lax.Precision.HIGHEST
 VMEM = pl.BlockSpec(memory_space=pltpu.VMEM)
 SMEM = pl.BlockSpec(memory_space=pltpu.SMEM)
@@ -131,7 +132,7 @@
     )(wanted, near(rows))
 
 
-def coef_kernel(diff_ref, mats_ref, own_ref, red_ref, diag_ref, own_t, row_t):
+def coef_kernel(diff_ref, mats_ref, own_ref, red_ref, top_ref, diag_ref, own_t, row_t):
     devices = red_ref.shape[1]
     row = lambda a, z: a[z : z + 1, :]
     lane = iota((1, LANES), 1)
@@ -175,14 +176,33 @@
     for kind, value in enumerate((left[0], left[-1], right[0], right[-1])):
         row_t[pl.ds(kind * devices, devices), :] = jnp.where(eye, value, 0.0)
     spread = jnp.dot(row_t[...], ones, precision=HIGH, preferred_element_type=jnp.float32)
-    ratio = jnp.zeros((1, LANES), jnp.float32)
+    none, all_of = jnp.zeros((1, LANES), jnp.float32), jnp.ones((1, LANES), jnp.float32)
+    groups = []
     for d in range(devices):
+        if d % GROUP == 0:
+            ratio, to_last, to_first, l_group = none, all_of, all_of, none
         l_first, l_last, r_first, r_last = (row(spread, kind * devices + d) for kind in range(4))
+        gain = 1.0 / (1.0 - l_first * ratio)
+        for kind, value in enumerate(
+            (
+                l_last * ratio * gain, l_last * gain, gain, gain * l_first, gain * r_first, ratio,
+                to_first * gain, to_first * gain * l_first,
+            )
+        ):
+            red_ref[kind, pl.ds(d, 1), :] = value
+        l_group = l_group + to_first * gain * l_first * to_last
+        to_first = to_first * gain * r_first
+        ratio = r_last + l_last * ratio * gain * r_first
+        to_last = l_last * gain * to_last
+        if d % GROUP == GROUP - 1:
+            groups.append((l_group, to_last, to_first, ratio))
+    ratio = none
+    for g, (l_first, l_last, r_first, r_last) in enumerate(groups):
         gain = 1.0 / (1.0 - l_first * ratio)
         for kind, value in enumerate(
             (l_last * ratio * gain, l_last * gain, gain, gain * l_first, gain * r_first, ratio)
         ):
-            red_ref[kind, pl.ds(d, 1), :] = value
+            top_ref[kind, pl.ds(g, 1), :] = value
         ratio = r_last + l_last * ratio * gain * r_first
     r, c = iota((LANES, LANES), 0), iota((LANES, LANES), 1)
     for kind, at in enumerate((r == c, r == c + 1, r == c - 1)):
@@ -201,11 +221,12 @@
         coef_kernel,
         out_shape=(
             pltpu.VMEM((5 * PLANES, LANES), jnp.float32),
-            pltpu.VMEM((6, devices, LANES), jnp.float32),
+            pltpu.VMEM((8, devices, LANES), jnp.float32),
+            pltpu.VMEM((6, devices // GROUP, LANES), jnp.float32),
             pltpu.VMEM((4 * NMAT, 3 * LANES), jnp.bfloat16),
         ),
         in_specs=[VMEM] * 2,
-        out_specs=[VMEM] * 3,
+        out_specs=[VMEM] * 4,
         scratch_shapes=[
             pltpu.VMEM((5 * PLANES, LANES), jnp.float32),
             pltpu.VMEM((4 * devices, LANES), jnp.float32),
@@ -340,12 +361,12 @@
         ends_ref[d, pl.ds(share, share), :] = last[d * share : (d + 1) * share, :]
 
 
-def slab(to, got, dep, weights, one, two, own, devices):
+def slab(to, got, dep, weights, one, two, own):
     base, ends, _ = pl.pallas_call(
         slab_kernel,
         out_shape=(
             pltpu.VMEM((TILES, LANES), jnp.float32),
-            pltpu.VMEM((devices, 2 * ROWS // devices, LANES), jnp.float32),
+            pltpu.VMEM((GROUP, 2 * ROWS // GROUP, LANES), jnp.float32),
             pltpu.VMEM((TILES + 8, LANES), jnp.float32),
         ),
         in_specs=[SMEM] + [VMEM] * 6,
@@ -358,34 +379,83 @@
     return base, ends
 
 
-def interface_kernel(ends_ref, red_ref, out_ref, carry_ref):
-    devices, both, _ = ends_ref.shape
-    share = both // 2
-    coef = lambda kind, d: red_ref[kind, pl.ds(d, 1), :]
-    upto = jnp.zeros((share, LANES), jnp.float32)
-    for d in range(devices):
-        first, last = ends_ref[d, pl.ds(0, share), :], ends_ref[d, pl.ds(share, share), :]
-        carry_ref[d] = upto
-        upto = last + coef(0, d) * first + coef(1, d) * upto
-    after = jnp.zeros((share, LANES), jnp.float32)
-    for d in range(devices - 1, -1, -1):
+def inner_kernel(ends_ref, red_ref, out_ref):
+    share = ends_ref.shape[1] // 2
+    start = lax.axis_index("gy") // GROUP * GROUP
+    coef = lambda kind, d: red_ref[kind, pl.ds(start + d, 1), :]
+    top = last = jnp.zeros((share, LANES), jnp.float32)
+    for d in range(GROUP):
         first = ends_ref[d, pl.ds(0, share), :]
-        out_ref[d, pl.ds(share, share), :] = after
-        after = coef(2, d) * first + coef(3, d) * carry_ref[d] + coef(4, d) * after
-        out_ref[d, pl.ds(0, share), :] = carry_ref[d] + coef(5, d) * after
-
-
-def interface(ends, red):
-    devices, both, _ = ends.shape
-    return pl.pallas_call(
-        interface_kernel,
-        out_shape=pltpu.VMEM(ends.shape, jnp.float32),
+        top = top + coef(6, d) * first + coef(7, d) * last
+        last = ends_ref[d, pl.ds(share, share), :] + coef(0, d) * first + coef(1, d) * last
+    for g in range(out_ref.shape[0]):
+        out_ref[g, pl.ds(0, share), :] = top
+        out_ref[g, pl.ds(share, share), :] = last
+
+
+def inner(ends, red, groups):
+    return pl.pallas_call(
+        inner_kernel,
+        out_shape=pltpu.VMEM((groups,) + ends.shape[1:], jnp.float32),
         in_specs=[VMEM] * 2,
         out_specs=VMEM,
-        scratch_shapes=[pltpu.VMEM((devices, both // 2, LANES), jnp.float32)],
-        compiler_params=PARAMS,
-        name="interface",
+        compiler_params=PARAMS,
+        name="inner",
     )(near(ends), near(red))
+
+
+def chain(ends_ref, coef, upto, after, carry_ref, put):
+    count, both, _ = ends_ref.shape
+    share = both // 2
+    for d in range(count):
+        first = ends_ref[d, pl.ds(0, share), :]
+        carry_ref[d] = upto
+        upto = ends_ref[d, pl.ds(share, share), :] + coef(0, d) * first + coef(1, d) * upto
+    for d in range(count - 1, -1, -1):
+        put(d, share, after)
+        after = coef(2, d) * ends_ref[d, pl.ds(0, share), :] + coef(3, d) * carry_ref[d] + coef(4, d) * after
+        put(d, 0, carry_ref[d] + coef(5, d) * after)
+
+
+def outer_kernel(ends_ref, groups_ref, red_ref, top_ref, out_ref, sides_ref, carry_ref):
+    share = ends_ref.shape[1] // 2
+    group = lax.axis_index("gy") // GROUP
+    zero = jnp.zeros((share, LANES), jnp.float32)
+
+    def put_group(g, at, value):
+        sides_ref[g, pl.ds(at, share), :] = value
+
+    chain(groups_ref, lambda kind, g: top_ref[kind, pl.ds(g, 1), :], zero, zero, carry_ref, put_group)
+
+    def put(d, at, value):
+        out_ref[d, pl.ds(at, share), :] = value
+
+    chain(
+        ends_ref, lambda kind, d: red_ref[kind, pl.ds(group * GROUP + d, 1), :],
+        sides_ref[group, pl.ds(0, share), :], sides_ref[group, pl.ds(share, share), :], carry_ref, put,
+    )
+
+
+def outer(ends, groups, red, top):
+    count, both, _ = ends.shape
+    return pl.pallas_call(
+        outer_kernel,
+        out_shape=pltpu.VMEM(ends.shape, jnp.float32),
+        in_specs=[VMEM] * 4,
+        out_specs=VMEM,
+        scratch_shapes=[
+            pltpu.VMEM(groups.shape, jnp.float32),
+            pltpu.VMEM((max(count, groups.shape[0]), both // 2, LANES), jnp.float32),
+        ],
+        compiler_params=PARAMS,
+        name="outer",
+    )(near(ends), near(groups), near(red), near(top))
+
+
+def exchanged(value, members):
+    return lax.all_to_all(
+        value, "gy", split_axis=0, concat_axis=0, tiled=True, axis_index_groups=members
+    )
 
 
 def finish_kernel(base_ref, near_ref, own_ref, out_ref, left_t, right_t):
@@ -421,17 +491,20 @@
     as_stored = lambda value: value.transpose(0, 2, 1)
     list1, list2, place, shift, rows = request(as_stored(src_shift), as_stored(src_tile), to_rows(conc))
     asked2, asked1 = shifted(list2, "gx", -2), shifted(list1, "gx", -1)
-    own, red, diag = coefficients(diffusivity, interp_mats, devices)
+    own, red, top, diag = coefficients(diffusivity, interp_mats, devices)
     got2 = shifted(serve(asked2, rows), "gx", 2)
     got1 = shifted(serve(asked1, rows), "gx", 1)
     dep, weights, to1, to2, one, two = before_arrival(
         place, rows, shift, as_stored(interp_class), diag, to_rows(target_one), to_rows(target_two)
     )
     dep = patched(to1, got1, dep)
-    base, ends = slab(to2, got2, dep, weights, one, two, own, devices)
-    ends = lax.all_to_all(ends, "gy", split_axis=0, concat_axis=0, tiled=True)
-    sides = interface(ends, red)
-    sides = lax.all_to_all(sides, "gy", split_axis=0, concat_axis=0, tiled=True)
+    base, ends = slab(to2, got2, dep, weights, one, two, own)
+    groups = devices // GROUP
+    close = [[g * GROUP + k for k in range(GROUP)] for g in range(groups)]
+    distant = [[g * GROUP + k for g in range(groups)] for k in range(GROUP)]
+    ends = exchanged(ends, close)
+    sides = outer(ends, exchanged(inner(ends, red, groups), distant), red, top)
+    sides = exchanged(sides, close)
     return from_rows(finish(base, sides, own), conc.shape)
 
 

time: 86.3 us -> 81 us (0.939)
  blocking collectives: 52.6 us -> 47.3 us
    all_to_all x2 -> x3, blocking collectives: 52.7 us -> 47.3 us  [exchanged(): lax.all_to_all(value, 'gy', split_axis=0, concat_axis=0, tiled=True, axis...]
where the time goes in v4:
time: 81 us; the launch traced here: 80.6 us
  blocking collectives  47.3 us (58%)
  Pallas kernels  16 us (20%)
  starting transfers between devices  14.3 us (18%)
  waiting for transfers between devices  2.76 us (3%)
    all_to_all x3, blocking collectives, exchanged(): lax.all_to_all(value, 'gy', split_axis=0, concat_axis=0, tiled=True, axis...  47.3 us
    ppermute x4, starting transfers between devices, shifted(): return lax.ppermute(value, axis, pairs)  14.3 us
    pallas_call x1, Pallas kernels, before_arrival(): pl.pallas_call(local_kernel, out_shape=(pltpu.VMEM((TILES + 8, LANES), jn...  4.47 us
    pallas_call x1, Pallas kernels, slab(): pl.pallas_call(slab_kernel, out_shape=(pltpu.VMEM((TILES, LANES), jnp.flo...  3.32 us
    ppermute x4, waiting for transfers between devices, shifted(): return lax.ppermute(value, axis, pairs)  2.76 us
    pallas_call x1, Pallas kernels, request(): pl.pallas_call(request_kernel, out_shape=(pltpu.VMEM((1, CAP), jnp.int32)...  2.64 us
    pallas_call x2, Pallas kernels, serve(): pl.pallas_call(serve_kernel, out_shape=pltpu.VMEM((CAP, LANES), jnp.float...  2.08 us
  transfers between devices with their start and end apart: 4, of which 2 were waited for; matrix products, arithmetic and copies ran while one was open for 0% of the time, Pallas kernels for 11%

profile of v4, /device:TPU:6, one launch (start us, length us, event | category | flops | bytes accessed | tf_op | source)
XLA Modules:
  0.0 80.6 jit_solution(17988144704259614240)
XLA Ops:
  0.0 2.6 %request.1 = (s32[1,512]{1,0:T(1,128)S(1)}, s32[1,512]{1,0:T(1,128)S(1)}, s32[16,128]{1,0:T(8,128)S(1)}, s32[16,128]{1,0:T(8,128)S(1)}, f32[2048,128]{1,0:T(8,128)S(1)}) custom-call(s32[16,8,16]{2,1,0:T(8,128)} %bitcast.29, s32[16,8,16]{2,1,0:T(8,128)} %bitcast.30, f32[2048,128]{1,0:T(8,128)} %bitcast.28), custom_call_target="tpu_custom_call" | custom-call | tf_op jit(solution)/shard_map/request/pallas_call | solution.py:97
  2.6 5.2 %collective-permute-start.2 = (s32[1,512]{1,0:T(1,128)S(1)}, s32[1,512]{1,0:T(1,128)S(1)}, u32[]{:S(2)}, u32[]{:S(2)}) collective-permute-start(s32[1,512]{1,0:T(1,128)S(1)} %get-tuple-element.29), channel_id=1, source_target_pairs={{32,0},{64,32},{96,64},{128,96},{160,128},{192,160},{224,192},{256... | collective-permute-start | bytes 6152 | tf_op jit(solution)/shard_map/ppermute | solution.py:29
  7.8 2.5 %collective-permute-start = (s32[1,512]{1,0:T(1,128)S(1)}, s32[1,512]{1,0:T(1,128)S(1)}, u32[]{:S(2)}, u32[]{:S(2)}) collective-permute-start(s32[1,512]{1,0:T(1,128)S(1)} %get-tuple-element.27), channel_id=1, source_target_pairs={{64,0},{96,32},{128,64},{160,96},{192,128},{224,160},{256,192},{28... | collective-permute-start | bytes 6152 | tf_op jit(solution)/shard_map/ppermute | solution.py:29
  10.4 0.0 collective-permute-done.2.list_ref
  10.4 0.0 copy-start
  10.4 0.0 copy-start.2
  10.4 1.0 %serve.3 = f32[512,128]{1,0:T(8,128)S(1)} custom-call(s32[1,512]{1,0:T(1,128)S(1)} %collective-permute-done.2.list_ref, f32[2048,128]{1,0:T(8,128)S(1)} %get-tuple-element.23.rows_ref), custom_call_target="tpu_custom_call" | custom-call | tf_op jit(solution)/shard_map/serve/pallas_call | solution.py:125
  11.5 0.0 copy-start.1
  11.5 3.0 %collective-permute-start.3 = (f32[512,128]{1,0:T(8,128)S(1)}, f32[512,128]{1,0:T(8,128)S(1)}, u32[]{:S(2)}, u32[]{:S(2)}) collective-permute-start(f32[512,128]{1,0:T(8,128)S(1)} %serve.3), channel_id=1, source_target_pairs={{0,32},{32,64},{64,96},{96,128},{128,160},{160,192},{192,224},{224... | collective-permute-start | bytes 786440 | tf_op jit(solution)/shard_map/ppermute | solution.py:29
  14.5 0.3 collective-permute-done.list_ref
  14.8 1.0 %serve.2 = f32[512,128]{1,0:T(8,128)S(1)} custom-call(s32[1,512]{1,0:T(1,128)S(1)} %collective-permute-done.list_ref, f32[2048,128]{1,0:T(8,128)S(1)} %get-tuple-element.23.rows_ref), custom_call_target="tpu_custom_call" | custom-call | tf_op jit(solution)/shard_map/serve/pallas_call | solution.py:125
  15.9 3.5 %collective-permute-start.1 = (f32[512,128]{1,0:T(8,128)S(1)}, f32[512,128]{1,0:T(8,128)S(1)}, u32[]{:S(2)}, u32[]{:S(2)}) collective-permute-start(f32[512,128]{1,0:T(8,128)S(1)} %serve.2), channel_id=1, source_target_pairs={{0,64},{32,96},{64,128},{96,160},{128,192},{160,224},{192,256},{22... | collective-permute-start | bytes 786440 | tf_op jit(solution)/shard_map/ppermute | solution.py:29
  19.4 0.0 copy-done
  19.4 1.3 %coefficients.1 = (f32[80,128]{1,0:T(8,128)S(1)}, f32[8,32,128]{2,1,0:T(8,128)S(1)}, f32[6,4,128]{2,1,0:T(4,128)S(1)}, bf16[32,384]{1,0:T(8,128)(2,1)S(1)}) custom-call(f32[4,128]{1,0:T(4,128)S(1)} %bitcast.25, f32[8,128,128]{2,1,0:T(8,128)S(1)} %copy-done), custom_call_target="tpu_custom_call" | custom-call | flops 8000000 | bytes 4000000 | tf_op jit(solution)/shard_map/coefficients/pallas_call | solution.py:220
  20.7 4.5 %before_arrival.1 = (f32[2056,128]{1,0:T(8,128)S(1)}, f32[2048,384]{1,0:T(8,128)S(1)}, s32[1,512]{1,0:T(1,128)S(1)}, s32[1,512]{1,0:T(1,128)S(1)}, f32[2048,128]{1,0:T(8,128)S(1)}, /*index=5*/f32[2048,128]{1,0:T(8,128)S(1)}) custom-call(s32[16,128]{1,0:T(8,128)S(1)} %get-tuple-element.22.place_ref, f32[2048,128]{1,0:T(8,128)S(1)} %get-tuple-element.23.rows_ref, ...), custom_call_target="tpu_custom_call" | custom-call | flops 20000000 | bytes 10000000 | tf_op jit(solution)/shard_map/before_arrival/pallas_call | solution.py:281
  25.2 0.0 collective-permute-done.3.got_ref
  25.2 1.0 %patch.1.dep_in = f32[2056,128]{1,0:T(8,128)S(1)} custom-call(s32[1,512]{1,0:T(1,128)S(1)} %get-tuple-element.28.to_ref, f32[512,128]{1,0:T(8,128)S(1)} %collective-permute-done.3.got_ref, f32[2056,128]{1,0:T(8,128)S(1)} %get-tuple-element.30.dep_in), custom_call_target="tpu_custom_call", output_to_operand_aliasing={{}: (2, {})} | custom-call | tf_op jit(solution)/shard_map/patch/pallas_call | solution.py:313
  26.3 2.4 %collective-permute-done.1.got_ref = f32[512,128]{1,0:T(8,128)S(1)} collective-permute-done((f32[512,128]{1,0:T(8,128)S(1)}, f32[512,128]{1,0:T(8,128)S(1)}, u32[]{:S(2)}, u32[]{:S(2)}) %collective-permute-start.1) | collective-permute-done | bytes 262176 | tf_op jit(solution)/shard_map/ppermute | solution.py:29
  28.7 3.3 %slab.1 = (f32[2048,128]{1,0:T(8,128)S(1)}, f32[8,32,128]{2,1,0:T(8,128)S(1)}, f32[2056,128]{1,0:T(8,128)S(1)}) custom-call(s32[1,512]{1,0:T(1,128)S(1)} %get-tuple-element.26.to_ref, f32[512,128]{1,0:T(8,128)S(1)} %collective-permute-done.1.got_ref, f32[2056,128]{1,0:T(8,128)S(1)} %patch.1.dep_in, ...), custom_call_target="tpu_custom_call", output_to_operand_aliasing={{2}: (2, {})} | custom-call | tf_op jit(solution)/shard_map/slab/pallas_call | solution.py:365
  32.0 12.5 %all_to_all.15.ends_ref = f32[8,32,128]{2,1,0:T(8,128)S(1)} all-to-all(f32[8,32,128]{2,1,0:T(8,128)S(1)} %get-tuple-element.36), channel_id=1, replica_groups={{0,1,2,3,4,5,6,7},{8,9,10,11,12,13,14,15},{16,17,18,19,20,21,22,23},{24..., dimensions={0} | all-to-all | bytes 262144 | tf_op jit(solution)/shard_map/all_to_all | solution.py:456
  44.6 25.2 %all_to_all.16.groups_ref = f32[4,32,128]{2,1,0:T(8,128)S(1)} all-to-all(f32[4,32,128]{2,1,0:T(8,128)S(1)} %inner.1), channel_id=1, replica_groups={{0,8,16,24},{1,9,17,25},{2,10,18,26},{3,11,19,27},{4,12,20,28},{5,13,21..., dimensions={0} | all-to-all | bytes 131072 | tf_op jit(solution)/shard_map/all_to_all | solution.py:456
  69.8 0.1 outer.1
  69.8 9.7 %all_to_all.17.near_ref = f32[8,32,128]{2,1,0:T(8,128)S(1)} all-to-all(f32[8,32,128]{2,1,0:T(8,128)S(1)} %outer.1), channel_id=1, replica_groups={{0,1,2,3,4,5,6,7},{8,9,10,11,12,13,14,15},{16,17,18,19,20,21,22,23},{24..., dimensions={0} | all-to-all | bytes 262144 | tf_op jit(solution)/shard_map/all_to_all | solution.py:456
  79.5 1.1 %finish.1 = f32[2048,128]{1,0:T(8,128)} custom-call(f32[2048,128]{1,0:T(8,128)S(1)} %get-tuple-element.35.base_ref, f32[8,32,128]{2,1,0:T(8,128)S(1)} %all_to_all.17.near_ref, f32[80,128]{1,0:T(8,128)S(1)} %get-tuple-element.34.own_ref), custom_call_target="tpu_custom_call" | custom-call | tf_op jit(solution)/shard_map/finish/pallas_call | solution.py:476
  (3 shorter events, 0.0 us)
Async XLA Ops:
  2.6 7.7 %collective-permute-start.2 = (s32[1,512]{1,0:T(1,128)S(1)}, s32[1,512]{1,0:T(1,128)S(1)}, u32[]{:S(2)}, u32[]{:S(2)}) collective-permute-start(s32[1,512]{1,0:T(1,128)S(1)} %get-tuple-element.29), channel_id=1, source_target_pairs={{32,0},{64,32},{96,64},{128,96},{160,128},{192,160},{224,192},{256... | collective-permute-start | bytes 6152 | tf_op jit(solution)/shard_map/ppermute | solution.py:29
  7.8 7.0 %collective-permute-start = (s32[1,512]{1,0:T(1,128)S(1)}, s32[1,512]{1,0:T(1,128)S(1)}, u32[]{:S(2)}, u32[]{:S(2)}) collective-permute-start(s32[1,512]{1,0:T(1,128)S(1)} %get-tuple-element.27), channel_id=1, source_target_pairs={{64,0},{96,32},{128,64},{160,96},{192,128},{224,160},{256,192},{28... | collective-permute-start | bytes 6152 | tf_op jit(solution)/shard_map/ppermute | solution.py:29
  10.4 9.0 %copy-start = (f32[8,128,128]{2,1,0:T(8,128)S(1)}, f32[8,128,128]{2,1,0:T(8,128)}, u32[]{:S(2)}) copy-start(f32[8,128,128]{2,1,0:T(8,128)} %mats_ref.1) | copy-start | bytes 1572868
  10.4 9.0 %copy-start.2 = (f32[512]{0:T(512)S(1)}, f32[512]{0:T(512)}, u32[]{:S(2)}) copy-start(f32[512]{0:T(512)} %param.11) | copy-start | bytes 6148
  11.5 9.3 %copy-start.1 = (s32[16,16,8]{1,2,0:T(8,128)S(1)}, s32[16,16,8]{1,2,0:T(8,128)}, u32[]{:S(2)}) copy-start(s32[16,16,8]{1,2,0:T(8,128)} %param.14) | copy-start | bytes 24580
  11.5 13.7 %collective-permute-start.3 = (f32[512,128]{1,0:T(8,128)S(1)}, f32[512,128]{1,0:T(8,128)S(1)}, u32[]{:S(2)}, u32[]{:S(2)}) collective-permute-start(f32[512,128]{1,0:T(8,128)S(1)} %serve.3), channel_id=1, source_target_pairs={{0,32},{32,64},{64,96},{96,128},{128,160},{160,192},{192,224},{224... | collective-permute-start | bytes 786440 | tf_op jit(solution)/shard_map/ppermute | solution.py:29
  15.9 12.8 %collective-permute-start.1 = (f32[512,128]{1,0:T(8,128)S(1)}, f32[512,128]{1,0:T(8,128)S(1)}, u32[]{:S(2)}, u32[]{:S(2)}) collective-permute-start(f32[512,128]{1,0:T(8,128)S(1)} %serve.2), channel_id=1, source_target_pairs={{0,64},{32,96},{64,128},{96,160},{128,192},{160,224},{192,256},{22... | collective-permute-start | bytes 786440 | tf_op jit(solution)/shard_map/ppermute | solution.py:29

commit v5 on v4

--- a/solution.py
+++ b/solution.py
@@ -53,29 +53,34 @@
     return jnp.concatenate([ref[:, b, :] for b in range(ref.shape[1])], axis=1)
 
 
-def ranks_of(mine):
+def compact(shift, value, empty, picked_ref):
     before_lane = (iota((LANES, LANES), 0) < iota((LANES, LANES), 1)).astype(jnp.bfloat16)
     before_row = (iota((PLANES, PLANES), 1) < iota((PLANES, PLANES), 0)).astype(jnp.bfloat16)
     all_lanes = jnp.ones((LANES, LANES), jnp.bfloat16)
-    mask = jnp.where(mine, 1.0, 0.0).astype(jnp.bfloat16)
-    inside = jnp.dot(mask, before_lane, preferred_element_type=jnp.float32)
-    per_row = jnp.dot(mask, all_lanes, preferred_element_type=jnp.float32)
-    ahead = jnp.dot(before_row, per_row.astype(jnp.bfloat16), preferred_element_type=jnp.float32)
-    return jnp.where(mine, (inside + ahead).astype(jnp.int32), -1)
-
-
-def compact(rank, value, empty, picked_ref):
-    for block in range(CAP // 64):
-        slot = iota((64, LANES), 0) + 64 * block
-        picked = jnp.zeros((64, LANES), jnp.float32)
-        for row in range(PLANES):
-            picked = jnp.where(rank[row : row + 1, :] == slot, value[row : row + 1, :] - empty, picked)
-        picked_ref[pl.ds(64 * block, 64), :] = picked
-    total = lax.dot_general(
-        jnp.ones((8, LANES), jnp.float32), picked_ref[...], (((1,), (1,)), ((), ())),
-        precision=HIGH, preferred_element_type=jnp.float32,
-    )
-    return (total[0:1, :] + empty).astype(jnp.int32)
+    for step in (1, 2):
+        mine = shift == step
+        mask = jnp.where(mine, 1.0, 0.0).astype(jnp.bfloat16)
+        inside = jnp.dot(mask, before_lane, preferred_element_type=jnp.float32)
+        per_row = jnp.dot(mask, all_lanes, preferred_element_type=jnp.float32)
+        ahead = jnp.dot(before_row, per_row.astype(jnp.bfloat16), preferred_element_type=jnp.float32)
+        rank = jnp.where(mine, (inside + ahead).astype(jnp.int32), -1)
+        for block in range(CAP // 64):
+            slot = iota((64, LANES), 0) + 64 * block
+            picked = jnp.zeros((64, LANES), jnp.int32)
+            for row in range(PLANES):
+                picked = jnp.where(
+                    rank[row : row + 1, :] == slot, value[row : row + 1, :] - empty, picked
+                )
+            picked_ref[pl.ds((step - 1) * CAP + 64 * block, 64), :] = picked
+    picked = picked_ref[...]
+    low = picked & 7
+    total = jnp.full((8, 2 * CAP), empty, jnp.float32)
+    for part in (picked - low, low):
+        total = total + lax.dot_general(
+            jnp.ones((8, LANES), jnp.bfloat16), part.astype(jnp.float32).astype(jnp.bfloat16),
+            (((1,), (1,)), ((), ())), preferred_element_type=jnp.float32,
+        )
+    return total[0:1, :].astype(jnp.int32)
 
 
 def request_kernel(
@@ -87,9 +92,9 @@
     place = (tile & -64) | ((tile & 7) << 3) | (lax.shift_right_logical(tile, 3) & 7)
     place_ref[...] = place
     shift_out[...] = shift
-    place = place.astype(jnp.float32)
-    for step, list_ref in ((1, list1_ref), (2, list2_ref)):
-        list_ref[...] = compact(ranks_of(shift == step), place, 0.0, picked_ref)
+    both = compact(shift, place, 0, picked_ref)
+    list1_ref[...] = both[:, :CAP]
+    list2_ref[...] = both[:, CAP:]
     copy.wait()
 
 
@@ -105,7 +110,7 @@
         ),
         in_specs=[VMEM] * 2 + [ANY],
         out_specs=[VMEM] * 5,
-        scratch_shapes=[pltpu.VMEM((CAP, LANES), jnp.float32), pltpu.SemaphoreType.DMA],
+        scratch_shapes=[pltpu.VMEM((2 * CAP, LANES), jnp.int32), pltpu.SemaphoreType.DMA],
         compiler_params=PARAMS,
         name="request",
     )(far(shift), far(tile), far(rows))
@@ -250,9 +255,9 @@
     shift = shift_ref[...]
     spot = iota((PLANES, LANES), 1)
     spot = ((spot & 8) << 3) | (lax.shift_right_logical(spot, 4) << 3) | (spot & 7)
-    spot = (spot + ROWS * iota((PLANES, LANES), 0)).astype(jnp.float32)
-    for step, to_ref in ((1, to1_ref), (2, to2_ref)):
-        to_ref[...] = compact(ranks_of(shift == step), spot, float(TILES), picked_ref)
+    both = compact(shift, spot + ROWS * iota((PLANES, LANES), 0), TILES, picked_ref)
+    to1_ref[...] = both[:, :CAP]
+    to2_ref[...] = both[:, CAP:]
     classes = by_lanes(class_ref)
     diag = diag_ref[...]
     of_class = jnp.bitwise_and(iota((4 * NMAT, ROWS), 0), NMAT - 1)
@@ -290,11 +295,16 @@
         ),
         in_specs=[SMEM] + [VMEM] * 4 + [ANY] * 2,
         out_specs=[VMEM] * 6,
-        scratch_shapes=[pltpu.VMEM((CAP, LANES), jnp.float32), pltpu.SemaphoreType.DMA((2,))],
+        scratch_shapes=[pltpu.VMEM((2 * CAP, LANES), jnp.int32), pltpu.SemaphoreType.DMA((2,))],
         compiler_params=PARAMS,
         cost_estimate=pl.CostEstimate(flops=20_000_000, bytes_accessed=10_000_000, transcendentals=0),
         name="before_arrival",
     )(place, near(rows), near(shift), classes, near(diag), far(one), far(two))
+
+
+def turned():
+    half = lax.axis_size("gy") // (2 * GROUP)
+    return jnp.where(lax.axis_index("gy") // GROUP >= half, GROUP // 2, 0)
 
 
 def patch_kernel(to_ref, got_ref, dep_in, dep_ref):
@@ -330,7 +340,7 @@
         return own_ref[pl.ds(kind * PLANES + z, 1), :]
 
     def forward(z, before):
-        here = pl.ds(pl.multiple_of(z * ROWS, ROWS), ROWS)
+        here = pl.ds(z * ROWS, ROWS)
         cells = dep_ref[here, :]
         adv = (
             weights_ref[here, pl.ds(0, LANES)] * cells
@@ -345,20 +355,25 @@
         partial[here, :] = before
         return before
 
-    last = lax.fori_loop(0, PLANES, forward, jnp.zeros((ROWS, LANES), jnp.float32))
+    last = jnp.zeros((ROWS, LANES), jnp.float32)
+    for z in range(PLANES):
+        last = forward(z, last)
 
     def backward(k, after):
         z = PLANES - 1 - k
-        here = pl.ds(pl.multiple_of(z * ROWS, ROWS), ROWS)
+        here = pl.ds(z * ROWS, ROWS)
         after = partial[here, :] + after * own(2, z)
         base_ref[here, :] = base_ref[here, :] + after
         return after
 
-    first = lax.fori_loop(0, PLANES, backward, jnp.zeros((ROWS, LANES), jnp.float32))
+    first = jnp.zeros((ROWS, LANES), jnp.float32)
+    for k in range(PLANES):
+        first = backward(k, first)
     share = ends_ref.shape[1] // 2
+    turn = turned()
     for d in range(ends_ref.shape[0]):
-        ends_ref[d, pl.ds(0, share), :] = first[d * share : (d + 1) * share, :]
-        ends_ref[d, pl.ds(share, share), :] = last[d * share : (d + 1) * share, :]
+        ends_ref[d ^ turn, pl.ds(0, share), :] = first[d * share : (d + 1) * share, :]
+        ends_ref[d ^ turn, pl.ds(share, share), :] = last[d * share : (d + 1) * share, :]
 
 
 def slab(to, got, dep, weights, one, two, own):
@@ -458,18 +473,26 @@
     )
 
 
-def finish_kernel(base_ref, near_ref, own_ref, out_ref, left_t, right_t):
+def finish_kernel(base_ref, near_ref, own_ref, out_hbm, left_t, right_t, out_t, sems):
     devices, both, _ = near_ref.shape
     share = both // 2
+    turn = turned()
     for d in range(devices):
-        left_t[pl.ds(d * share, share), :] = near_ref[d, pl.ds(0, share), :]
-        right_t[pl.ds(d * share, share), :] = near_ref[d, pl.ds(share, share), :]
+        left_t[pl.ds(d * share, share), :] = near_ref[d ^ turn, pl.ds(0, share), :]
+        right_t[pl.ds(d * share, share), :] = near_ref[d ^ turn, pl.ds(share, share), :]
     left, right = left_t[...], right_t[...]
+    copies = []
     for z in range(PLANES):
         here = pl.ds(z * ROWS, ROWS)
         from_left = own_ref[pl.ds(3 * PLANES + z, 1), :]
         from_right = own_ref[pl.ds(4 * PLANES + z, 1), :]
-        out_ref[here, :] = base_ref[here, :] + from_left * left + from_right * right
+        out_t[here, :] = base_ref[here, :] + from_left * left + from_right * right
+        if z % 4 == 3:
+            part = pl.ds((z - 3) * ROWS, 4 * ROWS)
+            copies.append(pltpu.make_async_copy(out_t.at[part], out_hbm.at[part], sems.at[z // 4]))
+            copies[-1].start()
+    for copy in copies:
+        copy.wait()
 
 
 def finish(base, sides, own):
@@ -477,8 +500,9 @@
         finish_kernel,
         out_shape=jax.ShapeDtypeStruct(base.shape, jnp.float32),
         in_specs=[VMEM] * 3,
-        out_specs=VMEM,
-        scratch_shapes=[pltpu.VMEM((ROWS, LANES), jnp.float32)] * 2,
+        out_specs=ANY,
+        scratch_shapes=[pltpu.VMEM((ROWS, LANES), jnp.float32)] * 2
+        + [pltpu.VMEM((TILES, LANES), jnp.float32), pltpu.SemaphoreType.DMA((PLANES // 4,))],
         compiler_params=PARAMS,
         name="finish",
     )(near(base), near(sides), near(own))
@@ -501,7 +525,8 @@
     base, ends = slab(to2, got2, dep, weights, one, two, own)
     groups = devices // GROUP
     close = [[g * GROUP + k for k in range(GROUP)] for g in range(groups)]
-    distant = [[g * GROUP + k for g in range(groups)] for k in range(GROUP)]
+    turn = [0 if g < groups // 2 else GROUP // 2 for g in range(groups)]
+    distant = [[g * GROUP + (k ^ turn[g]) for g in range(groups)] for k in range(GROUP)]
     ends = exchanged(ends, close)
     sides = outer(ends, exchanged(inner(ends, red, groups), distant), red, top)
     sides = exchanged(sides, close)

time: 81 us -> 76.6 us (0.946)
  blocking collectives: 47.3 us -> 44.8 us
  Pallas kernels: 16 us -> 13.6 us
    all_to_all x3, blocking collectives: 47.3 us -> 44.8 us  [exchanged(): lax.all_to_all(value, 'gy', split_axis=0, concat_axis=0, tiled=True, axis...]
    pallas_call x1, Pallas kernels: 3.32 us -> 2.01 us  [slab(): pl.pallas_call(slab_kernel, out_shape=(pltpu.VMEM((TILES, LANES), jnp.flo...]
  transfers between devices with their start and end apart: 4 -> 4, of which waited for: 2 -> 3; matrix products, arithmetic and copies ran while one was open for 0% -> 0% of each run, Pallas kernels for 11% -> 11%
where the time goes in v5:
time: 76.6 us; the launch traced here: 76.2 us
  blocking collectives  44.8 us (58%)
  starting transfers between devices  14.3 us (19%)
  Pallas kernels  13.6 us (18%)
  waiting for transfers between devices  3.28 us (4%)
    all_to_all x3, blocking collectives, exchanged(): lax.all_to_all(value, 'gy', split_axis=0, concat_axis=0, tiled=True, axis...  44.8 us
    ppermute x4, starting transfers between devices, shifted(): return lax.ppermute(value, axis, pairs)  14.3 us
    pallas_call x1, Pallas kernels, before_arrival(): pl.pallas_call(local_kernel, out_shape=(pltpu.VMEM((TILES + 8, LANES), jn...  3.96 us
    ppermute x4, waiting for transfers between devices, shifted(): return lax.ppermute(value, axis, pairs)  3.28 us
    pallas_call x1, Pallas kernels, request(): pl.pallas_call(request_kernel, out_shape=(pltpu.VMEM((1, CAP), jnp.int32)...  2.14 us
    pallas_call x2, Pallas kernels, serve(): pl.pallas_call(serve_kernel, out_shape=pltpu.VMEM((CAP, LANES), jnp.float...  2.08 us
    pallas_call x1, Pallas kernels, slab(): pl.pallas_call(slab_kernel, out_shape=(pltpu.VMEM((TILES, LANES), jnp.flo...  2.01 us
  transfers between devices with their start and end apart: 4, of which 3 were waited for; matrix products, arithmetic and copies ran while one was open for 0% of the time, Pallas kernels for 11%

profile of v5, /device:TPU:6, one launch (start us, length us, event | category | flops | bytes accessed | tf_op | source)
XLA Modules:
  0.0 76.2 jit_solution(8886208425999749112)
XLA Ops:
  0.0 2.1 %request.1 = (s32[1,512]{1,0:T(1,128)S(1)}, s32[1,512]{1,0:T(1,128)S(1)}, s32[16,128]{1,0:T(8,128)S(1)}, s32[16,128]{1,0:T(8,128)S(1)}, f32[2048,128]{1,0:T(8,128)S(1)}) custom-call(s32[16,8,16]{2,1,0:T(8,128)} %bitcast.29, s32[16,8,16]{2,1,0:T(8,128)} %bitcast.30, f32[2048,128]{1,0:T(8,128)} %bitcast.28), custom_call_target="tpu_custom_call" | custom-call | tf_op jit(solution)/shard_map/request/pallas_call | solution.py:102
  2.1 5.2 %collective-permute-start.2 = (s32[1,512]{1,0:T(1,128)S(1)}, s32[1,512]{1,0:T(1,128)S(1)}, u32[]{:S(2)}, u32[]{:S(2)}) collective-permute-start(s32[1,512]{1,0:T(1,128)S(1)} %get-tuple-element.29), channel_id=1, source_target_pairs={{32,0},{64,32},{96,64},{128,96},{160,128},{192,160},{224,192},{256... | collective-permute-start | bytes 6152 | tf_op jit(solution)/shard_map/ppermute | solution.py:29
  7.3 2.5 %collective-permute-start = (s32[1,512]{1,0:T(1,128)S(1)}, s32[1,512]{1,0:T(1,128)S(1)}, u32[]{:S(2)}, u32[]{:S(2)}) collective-permute-start(s32[1,512]{1,0:T(1,128)S(1)} %get-tuple-element.27), channel_id=1, source_target_pairs={{64,0},{96,32},{128,64},{160,96},{192,128},{224,160},{256,192},{28... | collective-permute-start | bytes 6152 | tf_op jit(solution)/shard_map/ppermute | solution.py:29
  9.9 0.0 collective-permute-done.2.list_ref
  9.9 0.0 copy-start
  9.9 0.0 copy-start.2
  9.9 1.0 %serve.3 = f32[512,128]{1,0:T(8,128)S(1)} custom-call(s32[1,512]{1,0:T(1,128)S(1)} %collective-permute-done.2.list_ref, f32[2048,128]{1,0:T(8,128)S(1)} %get-tuple-element.23.rows_ref), custom_call_target="tpu_custom_call" | custom-call | tf_op jit(solution)/shard_map/serve/pallas_call | solution.py:130
  11.0 0.0 copy-start.1
  11.0 3.0 %collective-permute-start.3 = (f32[512,128]{1,0:T(8,128)S(1)}, f32[512,128]{1,0:T(8,128)S(1)}, u32[]{:S(2)}, u32[]{:S(2)}) collective-permute-start(f32[512,128]{1,0:T(8,128)S(1)} %serve.3), channel_id=1, source_target_pairs={{0,32},{32,64},{64,96},{96,128},{128,160},{160,192},{192,224},{224... | collective-permute-start | bytes 786440 | tf_op jit(solution)/shard_map/ppermute | solution.py:29
  14.0 0.3 collective-permute-done.list_ref
  14.3 1.0 %serve.2 = f32[512,128]{1,0:T(8,128)S(1)} custom-call(s32[1,512]{1,0:T(1,128)S(1)} %collective-permute-done.list_ref, f32[2048,128]{1,0:T(8,128)S(1)} %get-tuple-element.23.rows_ref), custom_call_target="tpu_custom_call" | custom-call | tf_op jit(solution)/shard_map/serve/pallas_call | solution.py:130
  15.4 3.5 %collective-permute-start.1 = (f32[512,128]{1,0:T(8,128)S(1)}, f32[512,128]{1,0:T(8,128)S(1)}, u32[]{:S(2)}, u32[]{:S(2)}) collective-permute-start(f32[512,128]{1,0:T(8,128)S(1)} %serve.2), channel_id=1, source_target_pairs={{0,64},{32,96},{64,128},{96,160},{128,192},{160,224},{192,256},{22... | collective-permute-start | bytes 786440 | tf_op jit(solution)/shard_map/ppermute | solution.py:29
  18.9 0.0 copy-done
  18.9 1.3 %coefficients.1 = (f32[80,128]{1,0:T(8,128)S(1)}, f32[8,32,128]{2,1,0:T(8,128)S(1)}, f32[6,4,128]{2,1,0:T(4,128)S(1)}, bf16[32,384]{1,0:T(8,128)(2,1)S(1)}) custom-call(f32[4,128]{1,0:T(4,128)S(1)} %bitcast.25, f32[8,128,128]{2,1,0:T(8,128)S(1)} %copy-done), custom_call_target="tpu_custom_call" | custom-call | flops 8000000 | bytes 4000000 | tf_op jit(solution)/shard_map/coefficients/pallas_call | solution.py:225
  20.2 4.0 %before_arrival.1 = (f32[2056,128]{1,0:T(8,128)S(1)}, f32[2048,384]{1,0:T(8,128)S(1)}, s32[1,512]{1,0:T(1,128)S(1)}, s32[1,512]{1,0:T(1,128)S(1)}, f32[2048,128]{1,0:T(8,128)S(1)}, /*index=5*/f32[2048,128]{1,0:T(8,128)S(1)}) custom-call(s32[16,128]{1,0:T(8,128)S(1)} %get-tuple-element.22.place_ref, f32[2048,128]{1,0:T(8,128)S(1)} %get-tuple-element.23.rows_ref, ...), custom_call_target="tpu_custom_call" | custom-call | flops 20000000 | bytes 10000000 | tf_op jit(solution)/shard_map/before_arrival/pallas_call | solution.py:286
  24.2 0.2 collective-permute-done.3.got_ref
  24.4 1.0 %patch.1.dep_in = f32[2056,128]{1,0:T(8,128)S(1)} custom-call(s32[1,512]{1,0:T(1,128)S(1)} %get-tuple-element.28.to_ref, f32[512,128]{1,0:T(8,128)S(1)} %collective-permute-done.3.got_ref, f32[2056,128]{1,0:T(8,128)S(1)} %get-tuple-element.30.dep_in), custom_call_target="tpu_custom_call", output_to_operand_aliasing={{}: (2, {})} | custom-call | tf_op jit(solution)/shard_map/patch/pallas_call | solution.py:323
  25.5 2.8 %collective-permute-done.1.got_ref = f32[512,128]{1,0:T(8,128)S(1)} collective-permute-done((f32[512,128]{1,0:T(8,128)S(1)}, f32[512,128]{1,0:T(8,128)S(1)}, u32[]{:S(2)}, u32[]{:S(2)}) %collective-permute-start.1) | collective-permute-done | bytes 262176 | tf_op jit(solution)/shard_map/ppermute | solution.py:29
  28.2 2.0 %slab.1 = (f32[2048,128]{1,0:T(8,128)S(1)}, f32[8,32,128]{2,1,0:T(8,128)S(1)}, f32[2056,128]{1,0:T(8,128)S(1)}) custom-call(s32[1,512]{1,0:T(1,128)S(1)} %get-tuple-element.26.to_ref, f32[512,128]{1,0:T(8,128)S(1)} %collective-permute-done.1.got_ref, f32[2056,128]{1,0:T(8,128)S(1)} %patch.1.dep_in, ...), custom_call_target="tpu_custom_call", output_to_operand_aliasing={{2}: (2, {})} | custom-call | tf_op jit(solution)/shard_map/slab/pallas_call | solution.py:380
  30.2 12.5 %all_to_all.15.ends_ref = f32[8,32,128]{2,1,0:T(8,128)S(1)} all-to-all(f32[8,32,128]{2,1,0:T(8,128)S(1)} %get-tuple-element.36), channel_id=1, replica_groups={{0,1,2,3,4,5,6,7},{8,9,10,11,12,13,14,15},{16,17,18,19,20,21,22,23},{24..., dimensions={0} | all-to-all | bytes 262144 | tf_op jit(solution)/shard_map/all_to_all | solution.py:471
  42.7 21.7 %all_to_all.16.groups_ref = f32[4,32,128]{2,1,0:T(8,128)S(1)} all-to-all(f32[4,32,128]{2,1,0:T(8,128)S(1)} %inner.1), channel_id=1, replica_groups={{0,8,20,28},{1,9,21,29},{2,10,22,30},{3,11,23,31},{4,12,16,24},{5,13,17..., dimensions={0} | all-to-all | bytes 131072 | tf_op jit(solution)/shard_map/all_to_all | solution.py:471
  64.5 0.1 outer.1
  64.5 10.6 %all_to_all.17.near_ref = f32[8,32,128]{2,1,0:T(8,128)S(1)} all-to-all(f32[8,32,128]{2,1,0:T(8,128)S(1)} %outer.1), channel_id=1, replica_groups={{0,1,2,3,4,5,6,7},{8,9,10,11,12,13,14,15},{16,17,18,19,20,21,22,23},{24..., dimensions={0} | all-to-all | bytes 262144 | tf_op jit(solution)/shard_map/all_to_all | solution.py:471
  75.2 1.0 %finish.1 = f32[2048,128]{1,0:T(8,128)} custom-call(f32[2048,128]{1,0:T(8,128)S(1)} %get-tuple-element.35.base_ref, f32[8,32,128]{2,1,0:T(8,128)S(1)} %all_to_all.17.near_ref, f32[80,128]{1,0:T(8,128)S(1)} %get-tuple-element.34.own_ref), custom_call_target="tpu_custom_call" | custom-call | tf_op jit(solution)/shard_map/finish/pallas_call | solution.py:499
  (3 shorter events, 0.0 us)
Async XLA Ops:
  2.1 7.7 %collective-permute-start.2 = (s32[1,512]{1,0:T(1,128)S(1)}, s32[1,512]{1,0:T(1,128)S(1)}, u32[]{:S(2)}, u32[]{:S(2)}) collective-permute-start(s32[1,512]{1,0:T(1,128)S(1)} %get-tuple-element.29), channel_id=1, source_target_pairs={{32,0},{64,32},{96,64},{128,96},{160,128},{192,160},{224,192},{256... | collective-permute-start | bytes 6152 | tf_op jit(solution)/shard_map/ppermute | solution.py:29
  7.3 7.0 %collective-permute-start = (s32[1,512]{1,0:T(1,128)S(1)}, s32[1,512]{1,0:T(1,128)S(1)}, u32[]{:S(2)}, u32[]{:S(2)}) collective-permute-start(s32[1,512]{1,0:T(1,128)S(1)} %get-tuple-element.27), channel_id=1, source_target_pairs={{64,0},{96,32},{128,64},{160,96},{192,128},{224,160},{256,192},{28... | collective-permute-start | bytes 6152 | tf_op jit(solution)/shard_map/ppermute | solution.py:29
  9.9 9.0 %copy-start = (f32[8,128,128]{2,1,0:T(8,128)S(1)}, f32[8,128,128]{2,1,0:T(8,128)}, u32[]{:S(2)}) copy-start(f32[8,128,128]{2,1,0:T(8,128)} %mats_ref.1) | copy-start | bytes 1572868
  9.9 9.0 %copy-start.2 = (f32[512]{0:T(512)S(1)}, f32[512]{0:T(512)}, u32[]{:S(2)}) copy-start(f32[512]{0:T(512)} %param.11) | copy-start | bytes 6148
  11.0 9.3 %copy-start.1 = (s32[16,16,8]{1,2,0:T(8,128)S(1)}, s32[16,16,8]{1,2,0:T(8,128)}, u32[]{:S(2)}) copy-start(s32[16,16,8]{1,2,0:T(8,128)} %param.14) | copy-start | bytes 24580
  11.0 13.4 %collective-permute-start.3 = (f32[512,128]{1,0:T(8,128)S(1)}, f32[512,128]{1,0:T(8,128)S(1)}, u32[]{:S(2)}, u32[]{:S(2)}) collective-permute-start(f32[512,128]{1,0:T(8,128)S(1)} %serve.3), channel_id=1, source_target_pairs={{0,32},{32,64},{64,96},{96,128},{128,160},{160,192},{192,224},{224... | collective-permute-start | bytes 786440 | tf_op jit(solution)/shard_map/ppermute | solution.py:29
  15.4 12.8 %collective-permute-start.1 = (f32[512,128]{1,0:T(8,128)S(1)}, f32[512,128]{1,0:T(8,128)S(1)}, u32[]{:S(2)}, u32[]{:S(2)}) collective-permute-start(f32[512,128]{1,0:T(8,128)S(1)} %serve.2), channel_id=1, source_target_pairs={{0,64},{32,96},{64,128},{96,160},{128,192},{160,224},{192,256},{22... | collective-permute-start | bytes 786440 | tf_op jit(solution)/shard_map/ppermute | solution.py:29

commit v6 on v5

--- a/solution.py
+++ b/solution.py
@@ -244,7 +244,7 @@
 
 def local_kernel(
     place_ref, rows_ref, shift_ref, class_ref, diag_ref, one_hbm, two_hbm,
-    dep_ref, weights_ref, to1_ref, to2_ref, one_ref, two_ref, picked_ref, sems,
+    dep_ref, weights_ref, to1_ref, to2_ref, one_ref, two_ref, picked_ref, to_t, sems,
 ):
     copies = [
         pltpu.make_async_copy(one_hbm, one_ref, sems.at[0]),
@@ -256,8 +256,13 @@
     spot = iota((PLANES, LANES), 1)
     spot = ((spot & 8) << 3) | (lax.shift_right_logical(spot, 4) << 3) | (spot & 7)
     both = compact(shift, spot + ROWS * iota((PLANES, LANES), 0), TILES, picked_ref)
-    to1_ref[...] = both[:, :CAP]
-    to2_ref[...] = both[:, CAP:]
+    to_t[...] = both
+    copies = copies + [
+        pltpu.make_async_copy(to_t.at[:, pl.ds(0, CAP)], to1_ref, sems.at[2]),
+        pltpu.make_async_copy(to_t.at[:, pl.ds(CAP, CAP)], to2_ref, sems.at[3]),
+    ]
+    for copy in copies[2:]:
+        copy.start()
     classes = by_lanes(class_ref)
     diag = diag_ref[...]
     of_class = jnp.bitwise_and(iota((4 * NMAT, ROWS), 0), NMAT - 1)
@@ -288,14 +293,18 @@
         out_shape=(
             pltpu.VMEM((TILES + 8, LANES), jnp.float32),
             pltpu.VMEM((TILES, 3 * LANES), jnp.float32),
-            jax.ShapeDtypeStruct((1, CAP), jnp.int32),
-            jax.ShapeDtypeStruct((1, CAP), jnp.int32),
+            pltpu.SMEM((1, CAP), jnp.int32),
+            pltpu.SMEM((1, CAP), jnp.int32),
             pltpu.VMEM((TILES, LANES), jnp.float32),
             pltpu.VMEM((TILES, LANES), jnp.float32),
         ),
         in_specs=[SMEM] + [VMEM] * 4 + [ANY] * 2,
-        out_specs=[VMEM] * 6,
-        scratch_shapes=[pltpu.VMEM((2 * CAP, LANES), jnp.int32), pltpu.SemaphoreType.DMA((2,))],
+        out_specs=[VMEM] * 2 + [SMEM] * 2 + [VMEM] * 2,
+        scratch_shapes=[
+            pltpu.VMEM((2 * CAP, LANES), jnp.int32),
+            pltpu.VMEM((1, 2 * CAP), jnp.int32),
+            pltpu.SemaphoreType.DMA((4,)),
+        ],
         compiler_params=PARAMS,
         cost_estimate=pl.CostEstimate(flops=20_000_000, bytes_accessed=10_000_000, transcendentals=0),
         name="before_arrival",
@@ -328,7 +337,7 @@
         input_output_aliases={2: 0},
         compiler_params=PARAMS,
         name="patch",
-    )(to, near(got), near(dep))
+    )(pltpu.with_memory_space_constraint(to, pltpu.SMEM), near(got), near(dep))
 
 
 def slab_kernel(
@@ -390,7 +399,8 @@
         input_output_aliases={2: 2},
         compiler_params=PARAMS,
         name="slab",
-    )(to, near(got), near(dep), near(weights), near(one), near(two), near(own))
+    )(
+        pltpu.with_memory_space_constraint(to, pltpu.SMEM), near(got), near(dep), near(weights), near(one), near(two), near(own))
     return base, ends
 
 

time: 76.6 us -> 76.1 us (level)
  Pallas kernels: 13.6 us -> 12.6 us
  transfers between devices with their start and end apart: 4 -> 4, of which waited for: 3 -> 3; matrix products, arithmetic and copies ran while one was open for 0% -> 0% of each run, Pallas kernels for 11% -> 10%
where the time goes in v6:
time: 76.1 us; the launch traced here: 75.7 us
  blocking collectives  44.8 us (59%)
  starting transfers between devices  14.3 us (19%)
  Pallas kernels  12.6 us (17%)
  waiting for transfers between devices  3.82 us (5%)
    all_to_all x3, blocking collectives, exchanged(): lax.all_to_all(value, 'gy', split_axis=0, concat_axis=0, tiled=True, axis...  44.8 us
    ppermute x4, starting transfers between devices, shifted(): return lax.ppermute(value, axis, pairs)  14.3 us
    pallas_call x1, Pallas kernels, before_arrival(): pl.pallas_call(local_kernel, out_shape=(pltpu.VMEM((TILES + 8, LANES), jn...  4 us
    ppermute x4, waiting for transfers between devices, shifted(): return lax.ppermute(value, axis, pairs)  3.82 us
    pallas_call x1, Pallas kernels, request(): pl.pallas_call(request_kernel, out_shape=(pltpu.VMEM((1, CAP), jnp.int32)...  2.14 us
    pallas_call x2, Pallas kernels, serve(): pl.pallas_call(serve_kernel, out_shape=pltpu.VMEM((CAP, LANES), jnp.float...  2.08 us
  transfers between devices with their start and end apart: 4, of which 3 were waited for; matrix products, arithmetic and copies ran while one was open for 0% of the time, Pallas kernels for 10%

profile of v6, /device:TPU:6, one launch (start us, length us, event | category | flops | bytes accessed | tf_op | source)
XLA Modules:
  0.0 75.7 jit_solution(17993052354801336636)
XLA Ops:
  0.0 2.1 %request.1 = (s32[1,512]{1,0:T(1,128)S(1)}, s32[1,512]{1,0:T(1,128)S(1)}, s32[16,128]{1,0:T(8,128)S(1)}, s32[16,128]{1,0:T(8,128)S(1)}, f32[2048,128]{1,0:T(8,128)S(1)}) custom-call(s32[16,8,16]{2,1,0:T(8,128)} %bitcast.29, s32[16,8,16]{2,1,0:T(8,128)} %bitcast.30, f32[2048,128]{1,0:T(8,128)} %bitcast.28), custom_call_target="tpu_custom_call" | custom-call | tf_op jit(solution)/shard_map/request/pallas_call | solution.py:102
  2.1 5.2 %collective-permute-start.2 = (s32[1,512]{1,0:T(1,128)S(1)}, s32[1,512]{1,0:T(1,128)S(1)}, u32[]{:S(2)}, u32[]{:S(2)}) collective-permute-start(s32[1,512]{1,0:T(1,128)S(1)} %get-tuple-element.29), channel_id=1, source_target_pairs={{32,0},{64,32},{96,64},{128,96},{160,128},{192,160},{224,192},{256... | collective-permute-start | bytes 6152 | tf_op jit(solution)/shard_map/ppermute | solution.py:29
  7.3 2.5 %collective-permute-start = (s32[1,512]{1,0:T(1,128)S(1)}, s32[1,512]{1,0:T(1,128)S(1)}, u32[]{:S(2)}, u32[]{:S(2)}) collective-permute-start(s32[1,512]{1,0:T(1,128)S(1)} %get-tuple-element.27), channel_id=1, source_target_pairs={{64,0},{96,32},{128,64},{160,96},{192,128},{224,160},{256,192},{28... | collective-permute-start | bytes 6152 | tf_op jit(solution)/shard_map/ppermute | solution.py:29
  9.9 0.0 collective-permute-done.2.list_ref
  9.9 0.0 copy-start
  9.9 0.0 copy-start.2
  9.9 1.0 %serve.3 = f32[512,128]{1,0:T(8,128)S(1)} custom-call(s32[1,512]{1,0:T(1,128)S(1)} %collective-permute-done.2.list_ref, f32[2048,128]{1,0:T(8,128)S(1)} %get-tuple-element.23.rows_ref), custom_call_target="tpu_custom_call" | custom-call | tf_op jit(solution)/shard_map/serve/pallas_call | solution.py:130
  11.0 0.0 copy-start.1
  11.0 3.0 %collective-permute-start.3 = (f32[512,128]{1,0:T(8,128)S(1)}, f32[512,128]{1,0:T(8,128)S(1)}, u32[]{:S(2)}, u32[]{:S(2)}) collective-permute-start(f32[512,128]{1,0:T(8,128)S(1)} %serve.3), channel_id=1, source_target_pairs={{0,32},{32,64},{64,96},{96,128},{128,160},{160,192},{192,224},{224... | collective-permute-start | bytes 786440 | tf_op jit(solution)/shard_map/ppermute | solution.py:29
  14.0 0.3 collective-permute-done.list_ref
  14.3 1.0 %serve.2 = f32[512,128]{1,0:T(8,128)S(1)} custom-call(s32[1,512]{1,0:T(1,128)S(1)} %collective-permute-done.list_ref, f32[2048,128]{1,0:T(8,128)S(1)} %get-tuple-element.23.rows_ref), custom_call_target="tpu_custom_call" | custom-call | tf_op jit(solution)/shard_map/serve/pallas_call | solution.py:130
  15.4 3.5 %collective-permute-start.1 = (f32[512,128]{1,0:T(8,128)S(1)}, f32[512,128]{1,0:T(8,128)S(1)}, u32[]{:S(2)}, u32[]{:S(2)}) collective-permute-start(f32[512,128]{1,0:T(8,128)S(1)} %serve.2), channel_id=1, source_target_pairs={{0,64},{32,96},{64,128},{96,160},{128,192},{160,224},{192,256},{22... | collective-permute-start | bytes 786440 | tf_op jit(solution)/shard_map/ppermute | solution.py:29
  18.9 0.0 copy-done
  18.9 1.3 %coefficients.1 = (f32[80,128]{1,0:T(8,128)S(1)}, f32[8,32,128]{2,1,0:T(8,128)S(1)}, f32[6,4,128]{2,1,0:T(4,128)S(1)}, bf16[32,384]{1,0:T(8,128)(2,1)S(1)}) custom-call(f32[4,128]{1,0:T(4,128)S(1)} %bitcast.25, f32[8,128,128]{2,1,0:T(8,128)S(1)} %copy-done), custom_call_target="tpu_custom_call" | custom-call | flops 8000000 | bytes 4000000 | tf_op jit(solution)/shard_map/coefficients/pallas_call | solution.py:225
  20.2 4.0 %before_arrival.1 = (f32[2056,128]{1,0:T(8,128)S(1)}, f32[2048,384]{1,0:T(8,128)S(1)}, s32[1,512]{1,0:T(1,128)S(4)}, s32[1,512]{1,0:T(1,128)S(4)}, f32[2048,128]{1,0:T(8,128)S(1)}, /*index=5*/f32[2048,128]{1,0:T(8,128)S(1)}) custom-call(s32[16,128]{1,0:T(8,128)S(1)} %get-tuple-element.22.place_ref, f32[2048,128]{1,0:T(8,128)S(1)} %get-tuple-element.23.rows_ref, ...), custom_call_target="tpu_custom_call" | custom-call | flops 20000000 | bytes 10000000 | tf_op jit(solution)/shard_map/before_arrival/pallas_call | solution.py:291
  24.3 0.2 collective-permute-done.3.got_ref
  24.4 0.5 patch.1.dep_in
  24.9 3.3 %collective-permute-done.1.got_ref = f32[512,128]{1,0:T(8,128)S(1)} collective-permute-done((f32[512,128]{1,0:T(8,128)S(1)}, f32[512,128]{1,0:T(8,128)S(1)}, u32[]{:S(2)}, u32[]{:S(2)}) %collective-permute-start.1) | collective-permute-done | bytes 262176 | tf_op jit(solution)/shard_map/ppermute | solution.py:29
  28.2 1.5 %slab.1 = (f32[2048,128]{1,0:T(8,128)S(1)}, f32[8,32,128]{2,1,0:T(8,128)S(1)}, f32[2056,128]{1,0:T(8,128)S(1)}) custom-call(s32[1,512]{1,0:T(1,128)S(4)} %get-tuple-element.26.to_ref, f32[512,128]{1,0:T(8,128)S(1)} %collective-permute-done.1.got_ref, f32[2056,128]{1,0:T(8,128)S(1)} %patch.1.dep_in, ...), custom_call_target="tpu_custom_call", output_to_operand_aliasing={{2}: (2, {})} | custom-call | tf_op jit(solution)/shard_map/slab/pallas_call | solution.py:389
  29.7 12.5 %all_to_all.15.ends_ref = f32[8,32,128]{2,1,0:T(8,128)S(1)} all-to-all(f32[8,32,128]{2,1,0:T(8,128)S(1)} %get-tuple-element.36), channel_id=1, replica_groups={{0,1,2,3,4,5,6,7},{8,9,10,11,12,13,14,15},{16,17,18,19,20,21,22,23},{24..., dimensions={0} | all-to-all | bytes 262144 | tf_op jit(solution)/shard_map/all_to_all | solution.py:481
  42.2 21.7 %all_to_all.16.groups_ref = f32[4,32,128]{2,1,0:T(8,128)S(1)} all-to-all(f32[4,32,128]{2,1,0:T(8,128)S(1)} %inner.1), channel_id=1, replica_groups={{0,8,20,28},{1,9,21,29},{2,10,22,30},{3,11,23,31},{4,12,16,24},{5,13,17..., dimensions={0} | all-to-all | bytes 131072 | tf_op jit(solution)/shard_map/all_to_all | solution.py:481
  63.9 0.1 outer.1
  64.0 10.6 %all_to_all.17.near_ref = f32[8,32,128]{2,1,0:T(8,128)S(1)} all-to-all(f32[8,32,128]{2,1,0:T(8,128)S(1)} %outer.1), channel_id=1, replica_groups={{0,1,2,3,4,5,6,7},{8,9,10,11,12,13,14,15},{16,17,18,19,20,21,22,23},{24..., dimensions={0} | all-to-all | bytes 262144 | tf_op jit(solution)/shard_map/all_to_all | solution.py:481
  74.6 1.0 %finish.1 = f32[2048,128]{1,0:T(8,128)} custom-call(f32[2048,128]{1,0:T(8,128)S(1)} %get-tuple-element.35.base_ref, f32[8,32,128]{2,1,0:T(8,128)S(1)} %all_to_all.17.near_ref, f32[80,128]{1,0:T(8,128)S(1)} %get-tuple-element.34.own_ref), custom_call_target="tpu_custom_call" | custom-call | tf_op jit(solution)/shard_map/finish/pallas_call | solution.py:509
  (3 shorter events, 0.0 us)
Async XLA Ops:
  2.1 7.7 %collective-permute-start.2 = (s32[1,512]{1,0:T(1,128)S(1)}, s32[1,512]{1,0:T(1,128)S(1)}, u32[]{:S(2)}, u32[]{:S(2)}) collective-permute-start(s32[1,512]{1,0:T(1,128)S(1)} %get-tuple-element.29), channel_id=1, source_target_pairs={{32,0},{64,32},{96,64},{128,96},{160,128},{192,160},{224,192},{256... | collective-permute-start | bytes 6152 | tf_op jit(solution)/shard_map/ppermute | solution.py:29
  7.3 7.0 %collective-permute-start = (s32[1,512]{1,0:T(1,128)S(1)}, s32[1,512]{1,0:T(1,128)S(1)}, u32[]{:S(2)}, u32[]{:S(2)}) collective-permute-start(s32[1,512]{1,0:T(1,128)S(1)} %get-tuple-element.27), channel_id=1, source_target_pairs={{64,0},{96,32},{128,64},{160,96},{192,128},{224,160},{256,192},{28... | collective-permute-start | bytes 6152 | tf_op jit(solution)/shard_map/ppermute | solution.py:29
  9.9 9.0 %copy-start = (f32[8,128,128]{2,1,0:T(8,128)S(1)}, f32[8,128,128]{2,1,0:T(8,128)}, u32[]{:S(2)}) copy-start(f32[8,128,128]{2,1,0:T(8,128)} %mats_ref.1) | copy-start | bytes 1572868
  9.9 9.0 %copy-start.2 = (f32[512]{0:T(512)S(1)}, f32[512]{0:T(512)}, u32[]{:S(2)}) copy-start(f32[512]{0:T(512)} %param.11) | copy-start | bytes 6148
  11.0 9.3 %copy-start.1 = (s32[16,16,8]{1,2,0:T(8,128)S(1)}, s32[16,16,8]{1,2,0:T(8,128)}, u32[]{:S(2)}) copy-start(s32[16,16,8]{1,2,0:T(8,128)} %param.14) | copy-start | bytes 24580
  11.0 13.4 %collective-permute-start.3 = (f32[512,128]{1,0:T(8,128)S(1)}, f32[512,128]{1,0:T(8,128)S(1)}, u32[]{:S(2)}, u32[]{:S(2)}) collective-permute-start(f32[512,128]{1,0:T(8,128)S(1)} %serve.3), channel_id=1, source_target_pairs={{0,32},{32,64},{64,96},{96,128},{128,160},{160,192},{192,224},{224... | collective-permute-start | bytes 786440 | tf_op jit(solution)/shard_map/ppermute | solution.py:29
  15.4 12.8 %collective-permute-start.1 = (f32[512,128]{1,0:T(8,128)S(1)}, f32[512,128]{1,0:T(8,128)S(1)}, u32[]{:S(2)}, u32[]{:S(2)}) collective-permute-start(f32[512,128]{1,0:T(8,128)S(1)} %serve.2), channel_id=1, source_target_pairs={{0,64},{32,96},{64,128},{96,160},{128,192},{160,224},{192,256},{22... | collective-permute-start | bytes 786440 | tf_op jit(solution)/shard_map/ppermute | solution.py:29

commit v7 on v6

--- a/solution.py
+++ b/solution.py
@@ -84,11 +84,13 @@
 
 
 def request_kernel(
-    shift_ref, tile_ref, rows_hbm, list1_ref, list2_ref, place_ref, shift_out, rows_ref, picked_ref, sem
+    shift_ref, tile_ref, rows_hbm, list1_ref, list2_ref, place_ref, shift_out, rows_ref, code_ref, picked_ref, sem
 ):
     copy = pltpu.make_async_copy(rows_hbm, rows_ref, sem)
     copy.start()
-    shift, tile = by_lanes(shift_ref), by_lanes(tile_ref)
+    code_ref[...] = shift_ref[...] * TILES + tile_ref[...]
+    code = by_lanes(code_ref)
+    shift, tile = lax.shift_right_logical(code, 11), code & (TILES - 1)
     place = (tile & -64) | ((tile & 7) << 3) | (lax.shift_right_logical(tile, 3) & 7)
     place_ref[...] = place
     shift_out[...] = shift
@@ -110,7 +112,11 @@
         ),
         in_specs=[VMEM] * 2 + [ANY],
         out_specs=[VMEM] * 5,
-        scratch_shapes=[pltpu.VMEM((2 * CAP, LANES), jnp.int32), pltpu.SemaphoreType.DMA],
+        scratch_shapes=[
+            pltpu.VMEM(shift.shape, jnp.int32),
+            pltpu.VMEM((2 * CAP, LANES), jnp.int32),
+            pltpu.SemaphoreType.DMA,
+        ],
         compiler_params=PARAMS,
         name="request",
     )(far(shift), far(tile), far(rows))
@@ -118,12 +124,12 @@
 
 def serve_kernel(list_ref, rows_ref, out_ref):
     def step(k, carry):
-        for j in range(32):
-            slot = k * 32 + j
+        for j in range(128):
+            slot = k * 128 + j
             out_ref[pl.ds(slot, 1), :] = rows_ref[pl.ds(list_ref[0, slot], 1), :]
         return carry
 
-    lax.fori_loop(0, CAP // 32, step, 0)
+    lax.fori_loop(0, CAP // 128, step, 0)
 
 
 def serve(wanted, rows):

time: 76.1 us -> 75.9 us (level)
  no operation moved by 1% of the time
where the time goes in v7:
time: 75.9 us; the launch traced here: 75.5 us
  blocking collectives  44.8 us (59%)
  starting transfers between devices  14 us (18%)
  Pallas kernels  12.5 us (16%)
  waiting for transfers between devices  4.05 us (5%)
    all_to_all x3, blocking collectives, exchanged(): lax.all_to_all(value, 'gy', split_axis=0, concat_axis=0, tiled=True, axis...  44.8 us
    ppermute x4, starting transfers between devices, shifted(): return lax.ppermute(value, axis, pairs)  14 us
    ppermute x4, waiting for transfers between devices, shifted(): return lax.ppermute(value, axis, pairs)  4.05 us
    pallas_call x1, Pallas kernels, before_arrival(): pl.pallas_call(local_kernel, out_shape=(pltpu.VMEM((TILES + 8, LANES), jn...  4 us
    pallas_call x1, Pallas kernels, request(): pl.pallas_call(request_kernel, out_shape=(pltpu.VMEM((1, CAP), jnp.int32)...  2.15 us
    pallas_call x2, Pallas kernels, serve(): pl.pallas_call(serve_kernel, out_shape=pltpu.VMEM((CAP, LANES), jnp.float...  1.98 us
  transfers between devices with their start and end apart: 4, of which 3 were waited for; matrix products, arithmetic and copies ran while one was open for 0% of the time, Pallas kernels for 10%

profile of v7, /device:TPU:6, one launch (start us, length us, event | category | flops | bytes accessed | tf_op | source)
XLA Modules:
  0.0 75.5 jit_solution(1478223750121760670)
XLA Ops:
  0.0 2.1 %request.1 = (s32[1,512]{1,0:T(1,128)S(1)}, s32[1,512]{1,0:T(1,128)S(1)}, s32[16,128]{1,0:T(8,128)S(1)}, s32[16,128]{1,0:T(8,128)S(1)}, f32[2048,128]{1,0:T(8,128)S(1)}) custom-call(s32[16,8,16]{2,1,0:T(8,128)} %bitcast.29, s32[16,8,16]{2,1,0:T(8,128)} %bitcast.30, f32[2048,128]{1,0:T(8,128)} %bitcast.28), custom_call_target="tpu_custom_call" | custom-call | tf_op jit(solution)/shard_map/request/pallas_call | solution.py:104
  2.2 5.2 %collective-permute-start.2 = (s32[1,512]{1,0:T(1,128)S(1)}, s32[1,512]{1,0:T(1,128)S(1)}, u32[]{:S(2)}, u32[]{:S(2)}) collective-permute-start(s32[1,512]{1,0:T(1,128)S(1)} %get-tuple-element.29), channel_id=1, source_target_pairs={{32,0},{64,32},{96,64},{128,96},{160,128},{192,160},{224,192},{256... | collective-permute-start | bytes 6152 | tf_op jit(solution)/shard_map/ppermute | solution.py:29
  7.3 2.5 %collective-permute-start = (s32[1,512]{1,0:T(1,128)S(1)}, s32[1,512]{1,0:T(1,128)S(1)}, u32[]{:S(2)}, u32[]{:S(2)}) collective-permute-start(s32[1,512]{1,0:T(1,128)S(1)} %get-tuple-element.27), channel_id=1, source_target_pairs={{64,0},{96,32},{128,64},{160,96},{192,128},{224,160},{256,192},{28... | collective-permute-start | bytes 6152 | tf_op jit(solution)/shard_map/ppermute | solution.py:29
  9.9 0.0 collective-permute-done.2.list_ref
  9.9 0.0 copy-start
  9.9 0.0 copy-start.2
  9.9 1.0 %serve.3 = f32[512,128]{1,0:T(8,128)S(1)} custom-call(s32[1,512]{1,0:T(1,128)S(1)} %collective-permute-done.2.list_ref, f32[2048,128]{1,0:T(8,128)S(1)} %get-tuple-element.23.rows_ref), custom_call_target="tpu_custom_call" | custom-call | tf_op jit(solution)/shard_map/serve/pallas_call | solution.py:136
  10.9 0.0 copy-start.1
  10.9 2.9 %collective-permute-start.3 = (f32[512,128]{1,0:T(8,128)S(1)}, f32[512,128]{1,0:T(8,128)S(1)}, u32[]{:S(2)}, u32[]{:S(2)}) collective-permute-start(f32[512,128]{1,0:T(8,128)S(1)} %serve.3), channel_id=1, source_target_pairs={{0,32},{32,64},{64,96},{96,128},{128,160},{160,192},{192,224},{224... | collective-permute-start | bytes 786440 | tf_op jit(solution)/shard_map/ppermute | solution.py:29
  13.8 0.5 collective-permute-done.list_ref
  14.3 1.0 %serve.2 = f32[512,128]{1,0:T(8,128)S(1)} custom-call(s32[1,512]{1,0:T(1,128)S(1)} %collective-permute-done.list_ref, f32[2048,128]{1,0:T(8,128)S(1)} %get-tuple-element.23.rows_ref), custom_call_target="tpu_custom_call" | custom-call | tf_op jit(solution)/shard_map/serve/pallas_call | solution.py:136
  15.3 3.4 %collective-permute-start.1 = (f32[512,128]{1,0:T(8,128)S(1)}, f32[512,128]{1,0:T(8,128)S(1)}, u32[]{:S(2)}, u32[]{:S(2)}) collective-permute-start(f32[512,128]{1,0:T(8,128)S(1)} %serve.2), channel_id=1, source_target_pairs={{0,64},{32,96},{64,128},{96,160},{128,192},{160,224},{192,256},{22... | collective-permute-start | bytes 786440 | tf_op jit(solution)/shard_map/ppermute | solution.py:29
  18.7 0.0 copy-done
  18.7 1.3 %coefficients.1 = (f32[80,128]{1,0:T(8,128)S(1)}, f32[8,32,128]{2,1,0:T(8,128)S(1)}, f32[6,4,128]{2,1,0:T(4,128)S(1)}, bf16[32,384]{1,0:T(8,128)(2,1)S(1)}) custom-call(f32[4,128]{1,0:T(4,128)S(1)} %bitcast.25, f32[8,128,128]{2,1,0:T(8,128)S(1)} %copy-done), custom_call_target="tpu_custom_call" | custom-call | flops 8000000 | bytes 4000000 | tf_op jit(solution)/shard_map/coefficients/pallas_call | solution.py:231
  20.0 4.0 %before_arrival.1 = (f32[2056,128]{1,0:T(8,128)S(1)}, f32[2048,384]{1,0:T(8,128)S(1)}, s32[1,512]{1,0:T(1,128)S(4)}, s32[1,512]{1,0:T(1,128)S(4)}, f32[2048,128]{1,0:T(8,128)S(1)}, /*index=5*/f32[2048,128]{1,0:T(8,128)S(1)}) custom-call(s32[16,128]{1,0:T(8,128)S(1)} %get-tuple-element.22.place_ref, f32[2048,128]{1,0:T(8,128)S(1)} %get-tuple-element.23.rows_ref, ...), custom_call_target="tpu_custom_call" | custom-call | flops 20000000 | bytes 10000000 | tf_op jit(solution)/shard_map/before_arrival/pallas_call | solution.py:297
  24.0 0.3 collective-permute-done.3.got_ref
  24.3 0.5 patch.1.dep_in
  24.8 3.3 %collective-permute-done.1.got_ref = f32[512,128]{1,0:T(8,128)S(1)} collective-permute-done((f32[512,128]{1,0:T(8,128)S(1)}, f32[512,128]{1,0:T(8,128)S(1)}, u32[]{:S(2)}, u32[]{:S(2)}) %collective-permute-start.1) | collective-permute-done | bytes 262176 | tf_op jit(solution)/shard_map/ppermute | solution.py:29
  28.0 1.5 %slab.1 = (f32[2048,128]{1,0:T(8,128)S(1)}, f32[8,32,128]{2,1,0:T(8,128)S(1)}, f32[2056,128]{1,0:T(8,128)S(1)}) custom-call(s32[1,512]{1,0:T(1,128)S(4)} %get-tuple-element.26.to_ref, f32[512,128]{1,0:T(8,128)S(1)} %collective-permute-done.1.got_ref, f32[2056,128]{1,0:T(8,128)S(1)} %patch.1.dep_in, ...), custom_call_target="tpu_custom_call", output_to_operand_aliasing={{2}: (2, {})} | custom-call | tf_op jit(solution)/shard_map/slab/pallas_call | solution.py:395
  29.5 12.5 %all_to_all.15.ends_ref = f32[8,32,128]{2,1,0:T(8,128)S(1)} all-to-all(f32[8,32,128]{2,1,0:T(8,128)S(1)} %get-tuple-element.36), channel_id=1, replica_groups={{0,1,2,3,4,5,6,7},{8,9,10,11,12,13,14,15},{16,17,18,19,20,21,22,23},{24..., dimensions={0} | all-to-all | bytes 262144 | tf_op jit(solution)/shard_map/all_to_all | solution.py:487
  42.0 21.7 %all_to_all.16.groups_ref = f32[4,32,128]{2,1,0:T(8,128)S(1)} all-to-all(f32[4,32,128]{2,1,0:T(8,128)S(1)} %inner.1), channel_id=1, replica_groups={{0,8,20,28},{1,9,21,29},{2,10,22,30},{3,11,23,31},{4,12,16,24},{5,13,17..., dimensions={0} | all-to-all | bytes 131072 | tf_op jit(solution)/shard_map/all_to_all | solution.py:487
  63.8 0.1 outer.1
  63.8 10.6 %all_to_all.17.near_ref = f32[8,32,128]{2,1,0:T(8,128)S(1)} all-to-all(f32[8,32,128]{2,1,0:T(8,128)S(1)} %outer.1), channel_id=1, replica_groups={{0,1,2,3,4,5,6,7},{8,9,10,11,12,13,14,15},{16,17,18,19,20,21,22,23},{24..., dimensions={0} | all-to-all | bytes 262144 | tf_op jit(solution)/shard_map/all_to_all | solution.py:487
  74.5 1.0 %finish.1 = f32[2048,128]{1,0:T(8,128)} custom-call(f32[2048,128]{1,0:T(8,128)S(1)} %get-tuple-element.35.base_ref, f32[8,32,128]{2,1,0:T(8,128)S(1)} %all_to_all.17.near_ref, f32[80,128]{1,0:T(8,128)S(1)} %get-tuple-element.34.own_ref), custom_call_target="tpu_custom_call" | custom-call | tf_op jit(solution)/shard_map/finish/pallas_call | solution.py:515
  (3 shorter events, 0.0 us)
Async XLA Ops:
  2.2 7.7 %collective-permute-start.2 = (s32[1,512]{1,0:T(1,128)S(1)}, s32[1,512]{1,0:T(1,128)S(1)}, u32[]{:S(2)}, u32[]{:S(2)}) collective-permute-start(s32[1,512]{1,0:T(1,128)S(1)} %get-tuple-element.29), channel_id=1, source_target_pairs={{32,0},{64,32},{96,64},{128,96},{160,128},{192,160},{224,192},{256... | collective-permute-start | bytes 6152 | tf_op jit(solution)/shard_map/ppermute | solution.py:29
  7.3 7.0 %collective-permute-start = (s32[1,512]{1,0:T(1,128)S(1)}, s32[1,512]{1,0:T(1,128)S(1)}, u32[]{:S(2)}, u32[]{:S(2)}) collective-permute-start(s32[1,512]{1,0:T(1,128)S(1)} %get-tuple-element.27), channel_id=1, source_target_pairs={{64,0},{96,32},{128,64},{160,96},{192,128},{224,160},{256,192},{28... | collective-permute-start | bytes 6152 | tf_op jit(solution)/shard_map/ppermute | solution.py:29
  9.9 8.8 %copy-start = (f32[8,128,128]{2,1,0:T(8,128)S(1)}, f32[8,128,128]{2,1,0:T(8,128)}, u32[]{:S(2)}) copy-start(f32[8,128,128]{2,1,0:T(8,128)} %mats_ref.1) | copy-start | bytes 1572868
  9.9 8.8 %copy-start.2 = (f32[512]{0:T(512)S(1)}, f32[512]{0:T(512)}, u32[]{:S(2)}) copy-start(f32[512]{0:T(512)} %param.11) | copy-start | bytes 6148
  10.9 9.1 %copy-start.1 = (s32[16,16,8]{1,2,0:T(8,128)S(1)}, s32[16,16,8]{1,2,0:T(8,128)}, u32[]{:S(2)}) copy-start(s32[16,16,8]{1,2,0:T(8,128)} %param.14) | copy-start | bytes 24580
  10.9 13.4 %collective-permute-start.3 = (f32[512,128]{1,0:T(8,128)S(1)}, f32[512,128]{1,0:T(8,128)S(1)}, u32[]{:S(2)}, u32[]{:S(2)}) collective-permute-start(f32[512,128]{1,0:T(8,128)S(1)} %serve.3), channel_id=1, source_target_pairs={{0,32},{32,64},{64,96},{96,128},{128,160},{160,192},{192,224},{224... | collective-permute-start | bytes 786440 | tf_op jit(solution)/shard_map/ppermute | solution.py:29
  15.3 12.7 %collective-permute-start.1 = (f32[512,128]{1,0:T(8,128)S(1)}, f32[512,128]{1,0:T(8,128)S(1)}, u32[]{:S(2)}, u32[]{:S(2)}) collective-permute-start(f32[512,128]{1,0:T(8,128)S(1)} %serve.2), channel_id=1, source_target_pairs={{0,64},{32,96},{64,128},{96,160},{128,192},{160,224},{192,256},{22... | collective-permute-start | bytes 786440 | tf_op jit(solution)/shard_map/ppermute | solution.py:29
